TPU v7x, 512 devices: a whole 4x4x16 slice. The times are simulated.
512 devices in a mesh: layer: 8 (over x, core), rows: 64 (over z, y).
Axes of the slice: x: 4, y: 4, z: 16, core: 2. Of those that a mesh axis runs over, the one named last changes fastest.
Arguments:
- down_sources: bfloat16 [8, 32, 16384], P('layer', None, 'rows'), may hold values from -6 to 6
- up_sources: bfloat16 [8, 32, 16384], P('layer', None, 'rows'), may hold values from -6 to 6
- down_tiles: bfloat16 [8, 1024, 128, 128], P('layer', 'rows'), may hold values from -0.1875 to 0.1875
- up_tiles: bfloat16 [8, 1024, 128, 128], P('layer', 'rows'), may hold values from -0.1875 to 0.1875
- tile_rows: int32 [8, 1024], P('layer', 'rows'), may hold values from 0 to 127, as said below
- tile_cols: int32 [8, 1024], P('layer', 'rows'), may hold values from 0 to 127, as said below
- shot_order: int32 [32], replicated, may hold values from 0 to 31, each once
Outputs:
- traces: bfloat16 [8, 32, 16384], P('layer', None, 'rows')
Inputs may be any that keep to these rules, and one draw needn't show every extreme that they name: `tile_rows`: in every layer, tile t lies in the tile rows of index t // 16 of the rows axis: 2 * (t // 16) to 2 * (t // 16) + 1. `tile_cols`: every tile's column differs from its row by at most 2. `shot_order`: A permutation of the shots.
All inputs are finite; a program needn't handle non-finite values.
Results may differ from a plain program's by a relative error of at most 0.011.
Values may be sent and summed in bfloat16 or wider, within the bound.
A program may use at most 64 MiB of HBM per device.

v0:
```python
import jax
import jax.numpy as jnp
from jax import lax
from jax.sharding import PartitionSpec as P

TILE = 128


def padded(value, sides, width):
    for axis, dim in sides:
        devices, length = (lax.axis_size(axis), value.shape[dim])
        up = [(i, (i + 1) % devices) for i in range(devices - 1)]
        down = [(j, i) for i, j in up]
        last = lax.slice_in_dim(value, length - width, length, axis=dim)
        initial = lax.slice_in_dim(value, 0, width, axis=dim)
        before = lax.ppermute(last, axis, up)
        after = lax.ppermute(initial, axis, down)
        value = jnp.concatenate([before, value, after], axis=dim)
    return value


def from_behind(block, axis, distance):
    devices = range(lax.axis_size(axis))
    route = [(i - distance, i) for i in devices if i - distance in devices]
    return lax.ppermute(block, axis, route)


def widen_rows(trace):
    return padded(trace, (("rows", 2),), trace.shape[2])


def step_down(trace):
    return from_behind(trace, "layer", 1)


def step_up(trace):
    return from_behind(trace, "layer", -1)


def incoming_down(trace):
    return widen_rows(step_down(trace))


def incoming_up(trace):
    return widen_rows(step_up(trace))


def apply_layer(tiles, local_rows, cols, whole, first, count_rows):
    columns = whole.shape[1]
    blocks = whole[0].reshape(columns, -1, TILE)
    picked = jnp.take(blocks, cols - first, axis=1)
    product = jnp.einsum("tij,stj->sti", tiles, picked, preferred_element_type=jnp.float32)
    onehot = (local_rows[:, None] == jnp.arange(count_rows, dtype=jnp.int32)[None, :]).astype(
        jnp.float32
    )
    summed = jnp.einsum("sti,tr->sri", product, onehot, precision=lax.Precision.HIGHEST)
    return summed.reshape(1, columns, count_rows * TILE)


def advance(source, term):
    return (source.astype(jnp.float32) + term).astype(jnp.bfloat16)


def shards(down_sources, up_sources, down_tiles, up_tiles, tile_rows, tile_cols, shot_order):
    forward = jnp.take(down_sources, shot_order, axis=1)
    backward = jnp.take(up_sources, shot_order, axis=1)
    count_rows = forward.shape[2] // TILE
    local_rows = tile_rows[0] - lax.axis_index("rows") * count_rows
    first = (lax.axis_index("rows") - 1) * count_rows
    cols = tile_cols[0]
    turns = lax.axis_size("layer") - 1
    down_trace = forward
    up_trace = backward
    for turn in range(turns):
        whole = incoming_down(down_trace)
        down_trace = advance(
            forward, apply_layer(down_tiles[0], local_rows, cols, whole, first, count_rows)
        )
    for turn in range(turns):
        whole = incoming_up(up_trace)
        up_trace = advance(
            backward, apply_layer(up_tiles[0], local_rows, cols, whole, first, count_rows)
        )
    return (down_trace.astype(jnp.float32) + up_trace.astype(jnp.float32)).astype(jnp.bfloat16)


def solution(mesh):
    return jax.shard_map(
        shards,
        mesh=mesh,
        in_specs=(
            P("layer", None, "rows"),
            P("layer", None, "rows"),
            P("layer", "rows", None, None),
            P("layer", "rows", None, None),
            P("layer", "rows"),
            P("layer", "rows"),
            P(),
        ),
        out_specs=P("layer", None, "rows"),
        check_vma=False,
    )
```

profile of v0, /device:TPU:122, one launch (start us, length us, event | category | flops | bytes accessed | tf_op | source)
XLA Modules:
  0.0 197.2 jit_solution(980543000650631442)
XLA Ops:
  0.0 0.7 compare_select_fusion.1
  0.8 1.3 gather_fusion
  2.1 0.6 gather_fusion.8
  2.8 1.9 collective-permute-start
  4.7 3.6 %collective-permute-start.21 = (bf16[1,32,256]{2,1,0:T(8,128)(2,1)S(1)}, bf16[1,32,256]{2,1,0:T(8,128)(2,1)S(1)}, u32[]{:S(2)}, u32[]{:S(2)}) collective-permute-start(bf16[1,32,256]{2,1,0:T(8,128)(2,1)S(1)} %get-tuple-element.10), channel_id=1, source_target_pairs={{64,0},{128,64},{192,128},{256,192},{320,256},{384,320},{448,384},... | collective-permute-start | bytes 49160 | tf_op jit(solution)/shard_map/ppermute | solution.py:25
  8.4 0.6 copy-done.3
  9.1 0.6 copy-done.5
  9.7 4.7 %collective-permute-start.1 = (bf16[1,32,256]{2,1,0:T(8,128)(2,1)S(1)}, bf16[1,32,256]{2,1,0:T(8,128)(2,1)S(1)}, u32[]{:S(2)}, u32[]{:S(2)}) collective-permute-start(bf16[1,32,256]{2,1,0:T(8,128)(2,1)S(1)} %collective-permute-done), channel_id=1, source_target_pairs={{0,1},{1,2},{2,3},{3,4},{4,5},{5,6},{6,7},{7,8},{8,9},{9,10},{10,1... | collective-permute-start | bytes 49160 | tf_op jit(solution)/shard_map/ppermute | solution.py:16
  14.4 1.9 collective-permute-start.2
  16.4 7.2 %collective-permute-start.22 = (bf16[1,32,256]{2,1,0:T(8,128)(2,1)S(1)}, bf16[1,32,256]{2,1,0:T(8,128)(2,1)S(1)}, u32[]{:S(2)}, u32[]{:S(2)}) collective-permute-start(bf16[1,32,256]{2,1,0:T(8,128)(2,1)S(1)} %collective-permute-done.21), channel_id=1, source_target_pairs={{0,1},{1,2},{2,3},{3,4},{4,5},{5,6},{6,7},{7,8},{8,9},{9,10},{10,1... | collective-permute-start | bytes 49160 | tf_op jit(solution)/shard_map/ppermute | solution.py:16
  23.6 1.9 collective-permute-start.23
  25.7 0.6 gather_fusion.1
  27.1 1.9 collective-permute-start.3
  29.1 3.5 %collective-permute-done.23 = bf16[1,32,256]{2,1,0:T(8,128)(2,1)S(1)} collective-permute-done((bf16[1,32,256]{2,1,0:T(8,128)(2,1)S(1)}, bf16[1,32,256]{2,1,0:T(8,128)(2,1)S(1)}, u32[]{:S(2)}, u32[]{:S(2)}) %collective-permute-start.23) | collective-permute-done | bytes 16416 | tf_op jit(solution)/shard_map/ppermute | solution.py:17
  32.7 0.6 gather_fusion.9
  34.1 1.9 collective-permute-start.24
  36.0 5.5 %collective-permute-start.4 = (bf16[1,32,256]{2,1,0:T(8,128)(2,1)S(1)}, bf16[1,32,256]{2,1,0:T(8,128)(2,1)S(1)}, u32[]{:S(2)}, u32[]{:S(2)}) collective-permute-start(bf16[1,32,256]{2,1,0:T(8,128)(2,1)S(1)} %collective-permute-done.3), channel_id=1, source_target_pairs={{0,1},{1,2},{2,3},{3,4},{4,5},{5,6},{6,7},{7,8},{8,9},{9,10},{10,1... | collective-permute-start | bytes 49160 | tf_op jit(solution)/shard_map/ppermute | solution.py:16
  41.5 1.9 collective-permute-start.5
  43.5 7.2 %collective-permute-start.25 = (bf16[1,32,256]{2,1,0:T(8,128)(2,1)S(1)}, bf16[1,32,256]{2,1,0:T(8,128)(2,1)S(1)}, u32[]{:S(2)}, u32[]{:S(2)}) collective-permute-start(bf16[1,32,256]{2,1,0:T(8,128)(2,1)S(1)} %collective-permute-done.24), channel_id=1, source_target_pairs={{0,1},{1,2},{2,3},{3,4},{4,5},{5,6},{6,7},{7,8},{8,9},{9,10},{10,1... | collective-permute-start | bytes 49160 | tf_op jit(solution)/shard_map/ppermute | solution.py:16
  50.7 1.9 collective-permute-start.26
  52.8 0.6 gather_fusion.2
  54.2 1.9 collective-permute-start.6
  56.1 3.5 %collective-permute-done.26 = bf16[1,32,256]{2,1,0:T(8,128)(2,1)S(1)} collective-permute-done((bf16[1,32,256]{2,1,0:T(8,128)(2,1)S(1)}, bf16[1,32,256]{2,1,0:T(8,128)(2,1)S(1)}, u32[]{:S(2)}, u32[]{:S(2)}) %collective-permute-start.26) | collective-permute-done | bytes 16416 | tf_op jit(solution)/shard_map/ppermute | solution.py:17
  59.8 0.6 gather_fusion.10
  61.2 1.9 collective-permute-start.27
  63.1 5.5 %collective-permute-start.7 = (bf16[1,32,256]{2,1,0:T(8,128)(2,1)S(1)}, bf16[1,32,256]{2,1,0:T(8,128)(2,1)S(1)}, u32[]{:S(2)}, u32[]{:S(2)}) collective-permute-start(bf16[1,32,256]{2,1,0:T(8,128)(2,1)S(1)} %collective-permute-done.6), channel_id=1, source_target_pairs={{0,1},{1,2},{2,3},{3,4},{4,5},{5,6},{6,7},{7,8},{8,9},{9,10},{10,1... | collective-permute-start | bytes 49160 | tf_op jit(solution)/shard_map/ppermute | solution.py:16
  68.6 1.9 collective-permute-start.8
  70.6 7.2 %collective-permute-start.28 = (bf16[1,32,256]{2,1,0:T(8,128)(2,1)S(1)}, bf16[1,32,256]{2,1,0:T(8,128)(2,1)S(1)}, u32[]{:S(2)}, u32[]{:S(2)}) collective-permute-start(bf16[1,32,256]{2,1,0:T(8,128)(2,1)S(1)} %collective-permute-done.27), channel_id=1, source_target_pairs={{0,1},{1,2},{2,3},{3,4},{4,5},{5,6},{6,7},{7,8},{8,9},{9,10},{10,1... | collective-permute-start | bytes 49160 | tf_op jit(solution)/shard_map/ppermute | solution.py:16
  77.8 1.9 collective-permute-start.29
  79.9 0.6 gather_fusion.3
  81.3 1.9 collective-permute-start.9
  83.2 3.5 %collective-permute-done.29 = bf16[1,32,256]{2,1,0:T(8,128)(2,1)S(1)} collective-permute-done((bf16[1,32,256]{2,1,0:T(8,128)(2,1)S(1)}, bf16[1,32,256]{2,1,0:T(8,128)(2,1)S(1)}, u32[]{:S(2)}, u32[]{:S(2)}) %collective-permute-start.29) | collective-permute-done | bytes 16416 | tf_op jit(solution)/shard_map/ppermute | solution.py:17
  86.9 0.6 gather_fusion.11
  88.3 1.9 collective-permute-start.30
  90.2 5.5 %collective-permute-start.10 = (bf16[1,32,256]{2,1,0:T(8,128)(2,1)S(1)}, bf16[1,32,256]{2,1,0:T(8,128)(2,1)S(1)}, u32[]{:S(2)}, u32[]{:S(2)}) collective-permute-start(bf16[1,32,256]{2,1,0:T(8,128)(2,1)S(1)} %collective-permute-done.9), channel_id=1, source_target_pairs={{0,1},{1,2},{2,3},{3,4},{4,5},{5,6},{6,7},{7,8},{8,9},{9,10},{10,1... | collective-permute-start | bytes 49160 | tf_op jit(solution)/shard_map/ppermute | solution.py:16
  95.7 1.9 collective-permute-start.11
  97.6 7.2 %collective-permute-start.31 = (bf16[1,32,256]{2,1,0:T(8,128)(2,1)S(1)}, bf16[1,32,256]{2,1,0:T(8,128)(2,1)S(1)}, u32[]{:S(2)}, u32[]{:S(2)}) collective-permute-start(bf16[1,32,256]{2,1,0:T(8,128)(2,1)S(1)} %collective-permute-done.30), channel_id=1, source_target_pairs={{0,1},{1,2},{2,3},{3,4},{4,5},{5,6},{6,7},{7,8},{8,9},{9,10},{10,1... | collective-permute-start | bytes 49160 | tf_op jit(solution)/shard_map/ppermute | solution.py:16
  104.9 1.9 collective-permute-start.32
  107.0 0.6 gather_fusion.4
  108.4 1.9 collective-permute-start.12
  110.3 3.5 %collective-permute-done.32 = bf16[1,32,256]{2,1,0:T(8,128)(2,1)S(1)} collective-permute-done((bf16[1,32,256]{2,1,0:T(8,128)(2,1)S(1)}, bf16[1,32,256]{2,1,0:T(8,128)(2,1)S(1)}, u32[]{:S(2)}, u32[]{:S(2)}) %collective-permute-start.32) | collective-permute-done | bytes 16416 | tf_op jit(solution)/shard_map/ppermute | solution.py:17
  113.9 0.6 gather_fusion.12
  115.4 1.9 collective-permute-start.33
  117.3 5.5 %collective-permute-start.13 = (bf16[1,32,256]{2,1,0:T(8,128)(2,1)S(1)}, bf16[1,32,256]{2,1,0:T(8,128)(2,1)S(1)}, u32[]{:S(2)}, u32[]{:S(2)}) collective-permute-start(bf16[1,32,256]{2,1,0:T(8,128)(2,1)S(1)} %collective-permute-done.12), channel_id=1, source_target_pairs={{0,1},{1,2},{2,3},{3,4},{4,5},{5,6},{6,7},{7,8},{8,9},{9,10},{10,1... | collective-permute-start | bytes 49160 | tf_op jit(solution)/shard_map/ppermute | solution.py:16
  122.8 1.9 collective-permute-start.14
  124.7 7.2 %collective-permute-start.34 = (bf16[1,32,256]{2,1,0:T(8,128)(2,1)S(1)}, bf16[1,32,256]{2,1,0:T(8,128)(2,1)S(1)}, u32[]{:S(2)}, u32[]{:S(2)}) collective-permute-start(bf16[1,32,256]{2,1,0:T(8,128)(2,1)S(1)} %collective-permute-done.33), channel_id=1, source_target_pairs={{0,1},{1,2},{2,3},{3,4},{4,5},{5,6},{6,7},{7,8},{8,9},{9,10},{10,1... | collective-permute-start | bytes 49160 | tf_op jit(solution)/shard_map/ppermute | solution.py:16
  132.0 1.9 collective-permute-start.35
  134.0 0.6 gather_fusion.5
  135.5 1.9 collective-permute-start.15
  137.4 3.5 %collective-permute-done.35 = bf16[1,32,256]{2,1,0:T(8,128)(2,1)S(1)} collective-permute-done((bf16[1,32,256]{2,1,0:T(8,128)(2,1)S(1)}, bf16[1,32,256]{2,1,0:T(8,128)(2,1)S(1)}, u32[]{:S(2)}, u32[]{:S(2)}) %collective-permute-start.35) | collective-permute-done | bytes 16416 | tf_op jit(solution)/shard_map/ppermute | solution.py:17
  142.5 1.9 collective-permute-start.36
  144.4 5.5 %collective-permute-start.16 = (bf16[1,32,256]{2,1,0:T(8,128)(2,1)S(1)}, bf16[1,32,256]{2,1,0:T(8,128)(2,1)S(1)}, u32[]{:S(2)}, u32[]{:S(2)}) collective-permute-start(bf16[1,32,256]{2,1,0:T(8,128)(2,1)S(1)} %collective-permute-done.15), channel_id=1, source_target_pairs={{0,1},{1,2},{2,3},{3,4},{4,5},{5,6},{6,7},{7,8},{8,9},{9,10},{10,1... | collective-permute-start | bytes 49160 | tf_op jit(solution)/shard_map/ppermute | solution.py:16
  149.9 1.9 collective-permute-start.17
  151.8 7.2 %collective-permute-start.37 = (bf16[1,32,256]{2,1,0:T(8,128)(2,1)S(1)}, bf16[1,32,256]{2,1,0:T(8,128)(2,1)S(1)}, u32[]{:S(2)}, u32[]{:S(2)}) collective-permute-start(bf16[1,32,256]{2,1,0:T(8,128)(2,1)S(1)} %collective-permute-done.36), channel_id=1, source_target_pairs={{0,1},{1,2},{2,3},{3,4},{4,5},{5,6},{6,7},{7,8},{8,9},{9,10},{10,1... | collective-permute-start | bytes 49160 | tf_op jit(solution)/shard_map/ppermute | solution.py:16
  159.1 1.9 collective-permute-start.38
  162.6 1.9 collective-permute-start.18
  164.5 3.5 %collective-permute-done.38 = bf16[1,32,256]{2,1,0:T(8,128)(2,1)S(1)} collective-permute-done((bf16[1,32,256]{2,1,0:T(8,128)(2,1)S(1)}, bf16[1,32,256]{2,1,0:T(8,128)(2,1)S(1)}, u32[]{:S(2)}, u32[]{:S(2)}) %collective-permute-start.38) | collective-permute-done | bytes 16416 | tf_op jit(solution)/shard_map/ppermute | solution.py:17
  169.5 1.9 collective-permute-start.39
  171.5 5.5 %collective-permute-start.19 = (bf16[1,32,256]{2,1,0:T(8,128)(2,1)S(1)}, bf16[1,32,256]{2,1,0:T(8,128)(2,1)S(1)}, u32[]{:S(2)}, u32[]{:S(2)}) collective-permute-start(bf16[1,32,256]{2,1,0:T(8,128)(2,1)S(1)} %collective-permute-done.18), channel_id=1, source_target_pairs={{0,1},{1,2},{2,3},{3,4},{4,5},{5,6},{6,7},{7,8},{8,9},{9,10},{10,1... | collective-permute-start | bytes 49160 | tf_op jit(solution)/shard_map/ppermute | solution.py:16
  177.0 1.9 collective-permute-start.20
  178.9 7.2 %collective-permute-start.40 = (bf16[1,32,256]{2,1,0:T(8,128)(2,1)S(1)}, bf16[1,32,256]{2,1,0:T(8,128)(2,1)S(1)}, u32[]{:S(2)}, u32[]{:S(2)}) collective-permute-start(bf16[1,32,256]{2,1,0:T(8,128)(2,1)S(1)} %collective-permute-done.39), channel_id=1, source_target_pairs={{0,1},{1,2},{2,3},{3,4},{4,5},{5,6},{6,7},{7,8},{8,9},{9,10},{10,1... | collective-permute-start | bytes 49160 | tf_op jit(solution)/shard_map/ppermute | solution.py:16
  186.1 1.9 collective-permute-start.41
  189.6 5.5 %collective-permute-done.41 = bf16[1,32,256]{2,1,0:T(8,128)(2,1)S(1)} collective-permute-done((bf16[1,32,256]{2,1,0:T(8,128)(2,1)S(1)}, bf16[1,32,256]{2,1,0:T(8,128)(2,1)S(1)}, u32[]{:S(2)}, u32[]{:S(2)}) %collective-permute-start.41) | collective-permute-done | bytes 16416 | tf_op jit(solution)/shard_map/ppermute | solution.py:17
  196.6 0.6 add_convert_fusion
  (152 shorter events, 15.9 us)
Async XLA Ops:
  0.0 26.3 %copy-start = (bf16[1,16,128,128]{3,2,1,0:T(8,128)(2,1)S(1)}, bf16[1,16,128,128]{3,2,1,0:T(8,128)(2,1)}, u32[]{:S(2)}) copy-start(bf16[1,16,128,128]{3,2,1,0:T(8,128)(2,1)} %param.13) | copy-start | bytes 1572868
  0.0 0.7 copy-start.4
  0.8 1.3 copy-start.2
  2.8 6.9 %collective-permute-start = (bf16[1,32,256]{2,1,0:T(8,128)(2,1)S(1)}, bf16[1,32,256]{2,1,0:T(8,128)(2,1)S(1)}, u32[]{:S(2)}, u32[]{:S(2)}) collective-permute-start(bf16[1,32,256]{2,1,0:T(8,128)(2,1)S(1)} %get-tuple-element.9), channel_id=1, source_target_pairs={{0,64},{64,128},{128,192},{192,256},{256,320},{320,384},{384,448},... | collective-permute-start | bytes 49160 | tf_op jit(solution)/shard_map/ppermute | solution.py:25
  4.7 11.6 %collective-permute-start.21 = (bf16[1,32,256]{2,1,0:T(8,128)(2,1)S(1)}, bf16[1,32,256]{2,1,0:T(8,128)(2,1)S(1)}, u32[]{:S(2)}, u32[]{:S(2)}) collective-permute-start(bf16[1,32,256]{2,1,0:T(8,128)(2,1)S(1)} %get-tuple-element.10), channel_id=1, source_target_pairs={{64,0},{128,64},{192,128},{256,192},{320,256},{384,320},{448,384},... | collective-permute-start | bytes 49160 | tf_op jit(solution)/shard_map/ppermute | solution.py:25
  8.4 0.7 copy-start.3
  9.1 0.7 copy-start.5
  9.7 15.8 %collective-permute-start.1 = (bf16[1,32,256]{2,1,0:T(8,128)(2,1)S(1)}, bf16[1,32,256]{2,1,0:T(8,128)(2,1)S(1)}, u32[]{:S(2)}, u32[]{:S(2)}) collective-permute-start(bf16[1,32,256]{2,1,0:T(8,128)(2,1)S(1)} %collective-permute-done), channel_id=1, source_target_pairs={{0,1},{1,2},{2,3},{3,4},{4,5},{5,6},{6,7},{7,8},{8,9},{9,10},{10,1... | collective-permute-start | bytes 49160 | tf_op jit(solution)/shard_map/ppermute | solution.py:16
  14.4 11.1 %collective-permute-start.2 = (bf16[1,32,256]{2,1,0:T(8,128)(2,1)S(1)}, bf16[1,32,256]{2,1,0:T(8,128)(2,1)S(1)}, u32[]{:S(2)}, u32[]{:S(2)}) collective-permute-start(bf16[1,32,256]{2,1,0:T(8,128)(2,1)S(1)} %collective-permute-done), channel_id=1, source_target_pairs={{1,0},{2,1},{3,2},{4,3},{5,4},{6,5},{7,6},{8,7},{9,8},{10,9},{11,1... | collective-permute-start | bytes 49160 | tf_op jit(solution)/shard_map/ppermute | solution.py:17
  16.4 12.7 %collective-permute-start.22 = (bf16[1,32,256]{2,1,0:T(8,128)(2,1)S(1)}, bf16[1,32,256]{2,1,0:T(8,128)(2,1)S(1)}, u32[]{:S(2)}, u32[]{:S(2)}) collective-permute-start(bf16[1,32,256]{2,1,0:T(8,128)(2,1)S(1)} %collective-permute-done.21), channel_id=1, source_target_pairs={{0,1},{1,2},{2,3},{3,4},{4,5},{5,6},{6,7},{7,8},{8,9},{9,10},{10,1... | collective-permute-start | bytes 49160 | tf_op jit(solution)/shard_map/ppermute | solution.py:16
  23.6 9.0 %collective-permute-start.23 = (bf16[1,32,256]{2,1,0:T(8,128)(2,1)S(1)}, bf16[1,32,256]{2,1,0:T(8,128)(2,1)S(1)}, u32[]{:S(2)}, u32[]{:S(2)}) collective-permute-start(bf16[1,32,256]{2,1,0:T(8,128)(2,1)S(1)} %collective-permute-done.21), channel_id=1, source_target_pairs={{1,0},{2,1},{3,2},{4,3},{5,4},{6,5},{7,6},{8,7},{9,8},{10,9},{11,1... | collective-permute-start | bytes 49160 | tf_op jit(solution)/shard_map/ppermute | solution.py:17
  26.7 6.6 %copy-start.1 = (bf16[1,16,128,128]{3,2,1,0:T(8,128)(2,1)S(1)}, bf16[1,16,128,128]{3,2,1,0:T(8,128)(2,1)}, u32[]{:S(2)}) copy-start(bf16[1,16,128,128]{3,2,1,0:T(8,128)(2,1)} %param.14) | copy-start | bytes 1572868
  27.1 8.9 %collective-permute-start.3 = (bf16[1,32,256]{2,1,0:T(8,128)(2,1)S(1)}, bf16[1,32,256]{2,1,0:T(8,128)(2,1)S(1)}, u32[]{:S(2)}, u32[]{:S(2)}) collective-permute-start(bf16[1,32,256]{2,1,0:T(8,128)(2,1)S(1)} %fusion.112), channel_id=1, source_target_pairs={{0,64},{64,128},{128,192},{192,256},{256,320},{320,384},{384,448},... | collective-permute-start | bytes 49160 | tf_op jit(solution)/shard_map/ppermute | solution.py:25
  34.1 9.4 %collective-permute-start.24 = (bf16[1,32,256]{2,1,0:T(8,128)(2,1)S(1)}, bf16[1,32,256]{2,1,0:T(8,128)(2,1)S(1)}, u32[]{:S(2)}, u32[]{:S(2)}) collective-permute-start(bf16[1,32,256]{2,1,0:T(8,128)(2,1)S(1)} %fusion.119), channel_id=1, source_target_pairs={{64,0},{128,64},{192,128},{256,192},{320,256},{384,320},{448,384},... | collective-permute-start | bytes 49160 | tf_op jit(solution)/shard_map/ppermute | solution.py:25
  36.0 16.6 %collective-permute-start.4 = (bf16[1,32,256]{2,1,0:T(8,128)(2,1)S(1)}, bf16[1,32,256]{2,1,0:T(8,128)(2,1)S(1)}, u32[]{:S(2)}, u32[]{:S(2)}) collective-permute-start(bf16[1,32,256]{2,1,0:T(8,128)(2,1)S(1)} %collective-permute-done.3), channel_id=1, source_target_pairs={{0,1},{1,2},{2,3},{3,4},{4,5},{5,6},{6,7},{7,8},{8,9},{9,10},{10,1... | collective-permute-start | bytes 49160 | tf_op jit(solution)/shard_map/ppermute | solution.py:16
  41.5 11.1 %collective-permute-start.5 = (bf16[1,32,256]{2,1,0:T(8,128)(2,1)S(1)}, bf16[1,32,256]{2,1,0:T(8,128)(2,1)S(1)}, u32[]{:S(2)}, u32[]{:S(2)}) collective-permute-start(bf16[1,32,256]{2,1,0:T(8,128)(2,1)S(1)} %collective-permute-done.3), channel_id=1, source_target_pairs={{1,0},{2,1},{3,2},{4,3},{5,4},{6,5},{7,6},{8,7},{9,8},{10,9},{11,1... | collective-permute-start | bytes 49160 | tf_op jit(solution)/shard_map/ppermute | solution.py:17
  43.5 12.7 %collective-permute-start.25 = (bf16[1,32,256]{2,1,0:T(8,128)(2,1)S(1)}, bf16[1,32,256]{2,1,0:T(8,128)(2,1)S(1)}, u32[]{:S(2)}, u32[]{:S(2)}) collective-permute-start(bf16[1,32,256]{2,1,0:T(8,128)(2,1)S(1)} %collective-permute-done.24), channel_id=1, source_target_pairs={{0,1},{1,2},{2,3},{3,4},{4,5},{5,6},{6,7},{7,8},{8,9},{9,10},{10,1... | collective-permute-start | bytes 49160 | tf_op jit(solution)/shard_map/ppermute | solution.py:16
  50.7 9.0 %collective-permute-start.26 = (bf16[1,32,256]{2,1,0:T(8,128)(2,1)S(1)}, bf16[1,32,256]{2,1,0:T(8,128)(2,1)S(1)}, u32[]{:S(2)}, u32[]{:S(2)}) collective-permute-start(bf16[1,32,256]{2,1,0:T(8,128)(2,1)S(1)} %collective-permute-done.24), channel_id=1, source_target_pairs={{1,0},{2,1},{3,2},{4,3},{5,4},{6,5},{7,6},{8,7},{9,8},{10,9},{11,1... | collective-permute-start | bytes 49160 | tf_op jit(solution)/shard_map/ppermute | solution.py:17
  54.2 8.9 %collective-permute-start.6 = (bf16[1,32,256]{2,1,0:T(8,128)(2,1)S(1)}, bf16[1,32,256]{2,1,0:T(8,128)(2,1)S(1)}, u32[]{:S(2)}, u32[]{:S(2)}) collective-permute-start(bf16[1,32,256]{2,1,0:T(8,128)(2,1)S(1)} %fusion.113), channel_id=1, source_target_pairs={{0,64},{64,128},{128,192},{192,256},{256,320},{320,384},{384,448},... | collective-permute-start | bytes 49160 | tf_op jit(solution)/shard_map/ppermute | solution.py:25
  61.2 9.3 %collective-permute-start.27 = (bf16[1,32,256]{2,1,0:T(8,128)(2,1)S(1)}, bf16[1,32,256]{2,1,0:T(8,128)(2,1)S(1)}, u32[]{:S(2)}, u32[]{:S(2)}) collective-permute-start(bf16[1,32,256]{2,1,0:T(8,128)(2,1)S(1)} %fusion.120), channel_id=1, source_target_pairs={{64,0},{128,64},{192,128},{256,192},{320,256},{384,320},{448,384},... | collective-permute-start | bytes 49160 | tf_op jit(solution)/shard_map/ppermute | solution.py:25
  63.1 16.6 %collective-permute-start.7 = (bf16[1,32,256]{2,1,0:T(8,128)(2,1)S(1)}, bf16[1,32,256]{2,1,0:T(8,128)(2,1)S(1)}, u32[]{:S(2)}, u32[]{:S(2)}) collective-permute-start(bf16[1,32,256]{2,1,0:T(8,128)(2,1)S(1)} %collective-permute-done.6), channel_id=1, source_target_pairs={{0,1},{1,2},{2,3},{3,4},{4,5},{5,6},{6,7},{7,8},{8,9},{9,10},{10,1... | collective-permute-start | bytes 49160 | tf_op jit(solution)/shard_map/ppermute | solution.py:16
  68.6 11.1 %collective-permute-start.8 = (bf16[1,32,256]{2,1,0:T(8,128)(2,1)S(1)}, bf16[1,32,256]{2,1,0:T(8,128)(2,1)S(1)}, u32[]{:S(2)}, u32[]{:S(2)}) collective-permute-start(bf16[1,32,256]{2,1,0:T(8,128)(2,1)S(1)} %collective-permute-done.6), channel_id=1, source_target_pairs={{1,0},{2,1},{3,2},{4,3},{5,4},{6,5},{7,6},{8,7},{9,8},{10,9},{11,1... | collective-permute-start | bytes 49160 | tf_op jit(solution)/shard_map/ppermute | solution.py:17
  70.6 12.7 %collective-permute-start.28 = (bf16[1,32,256]{2,1,0:T(8,128)(2,1)S(1)}, bf16[1,32,256]{2,1,0:T(8,128)(2,1)S(1)}, u32[]{:S(2)}, u32[]{:S(2)}) collective-permute-start(bf16[1,32,256]{2,1,0:T(8,128)(2,1)S(1)} %collective-permute-done.27), channel_id=1, source_target_pairs={{0,1},{1,2},{2,3},{3,4},{4,5},{5,6},{6,7},{7,8},{8,9},{9,10},{10,1... | collective-permute-start | bytes 49160 | tf_op jit(solution)/shard_map/ppermute | solution.py:16
  77.8 9.0 %collective-permute-start.29 = (bf16[1,32,256]{2,1,0:T(8,128)(2,1)S(1)}, bf16[1,32,256]{2,1,0:T(8,128)(2,1)S(1)}, u32[]{:S(2)}, u32[]{:S(2)}) collective-permute-start(bf16[1,32,256]{2,1,0:T(8,128)(2,1)S(1)} %collective-permute-done.27), channel_id=1, source_target_pairs={{1,0},{2,1},{3,2},{4,3},{5,4},{6,5},{7,6},{8,7},{9,8},{10,9},{11,1... | collective-permute-start | bytes 49160 | tf_op jit(solution)/shard_map/ppermute | solution.py:17
  81.3 8.9 %collective-permute-start.9 = (bf16[1,32,256]{2,1,0:T(8,128)(2,1)S(1)}, bf16[1,32,256]{2,1,0:T(8,128)(2,1)S(1)}, u32[]{:S(2)}, u32[]{:S(2)}) collective-permute-start(bf16[1,32,256]{2,1,0:T(8,128)(2,1)S(1)} %fusion.114), channel_id=1, source_target_pairs={{0,64},{64,128},{128,192},{192,256},{256,320},{320,384},{384,448},... | collective-permute-start | bytes 49160 | tf_op jit(solution)/shard_map/ppermute | solution.py:25
  88.3 9.3 %collective-permute-start.30 = (bf16[1,32,256]{2,1,0:T(8,128)(2,1)S(1)}, bf16[1,32,256]{2,1,0:T(8,128)(2,1)S(1)}, u32[]{:S(2)}, u32[]{:S(2)}) collective-permute-start(bf16[1,32,256]{2,1,0:T(8,128)(2,1)S(1)} %fusion.121), channel_id=1, source_target_pairs={{64,0},{128,64},{192,128},{256,192},{320,256},{384,320},{448,384},... | collective-permute-start | bytes 49160 | tf_op jit(solution)/shard_map/ppermute | solution.py:25
  90.2 16.6 %collective-permute-start.10 = (bf16[1,32,256]{2,1,0:T(8,128)(2,1)S(1)}, bf16[1,32,256]{2,1,0:T(8,128)(2,1)S(1)}, u32[]{:S(2)}, u32[]{:S(2)}) collective-permute-start(bf16[1,32,256]{2,1,0:T(8,128)(2,1)S(1)} %collective-permute-done.9), channel_id=1, source_target_pairs={{0,1},{1,2},{2,3},{3,4},{4,5},{5,6},{6,7},{7,8},{8,9},{9,10},{10,1... | collective-permute-start | bytes 49160 | tf_op jit(solution)/shard_map/ppermute | solution.py:16
  95.7 11.1 %collective-permute-start.11 = (bf16[1,32,256]{2,1,0:T(8,128)(2,1)S(1)}, bf16[1,32,256]{2,1,0:T(8,128)(2,1)S(1)}, u32[]{:S(2)}, u32[]{:S(2)}) collective-permute-start(bf16[1,32,256]{2,1,0:T(8,128)(2,1)S(1)} %collective-permute-done.9), channel_id=1, source_target_pairs={{1,0},{2,1},{3,2},{4,3},{5,4},{6,5},{7,6},{8,7},{9,8},{10,9},{11,1... | collective-permute-start | bytes 49160 | tf_op jit(solution)/shard_map/ppermute | solution.py:17
  97.6 12.7 %collective-permute-start.31 = (bf16[1,32,256]{2,1,0:T(8,128)(2,1)S(1)}, bf16[1,32,256]{2,1,0:T(8,128)(2,1)S(1)}, u32[]{:S(2)}, u32[]{:S(2)}) collective-permute-start(bf16[1,32,256]{2,1,0:T(8,128)(2,1)S(1)} %collective-permute-done.30), channel_id=1, source_target_pairs={{0,1},{1,2},{2,3},{3,4},{4,5},{5,6},{6,7},{7,8},{8,9},{9,10},{10,1... | collective-permute-start | bytes 49160 | tf_op jit(solution)/shard_map/ppermute | solution.py:16
  104.9 9.0 %collective-permute-start.32 = (bf16[1,32,256]{2,1,0:T(8,128)(2,1)S(1)}, bf16[1,32,256]{2,1,0:T(8,128)(2,1)S(1)}, u32[]{:S(2)}, u32[]{:S(2)}) collective-permute-start(bf16[1,32,256]{2,1,0:T(8,128)(2,1)S(1)} %collective-permute-done.30), channel_id=1, source_target_pairs={{1,0},{2,1},{3,2},{4,3},{5,4},{6,5},{7,6},{8,7},{9,8},{10,9},{11,1... | collective-permute-start | bytes 49160 | tf_op jit(solution)/shard_map/ppermute | solution.py:17
  108.4 8.9 %collective-permute-start.12 = (bf16[1,32,256]{2,1,0:T(8,128)(2,1)S(1)}, bf16[1,32,256]{2,1,0:T(8,128)(2,1)S(1)}, u32[]{:S(2)}, u32[]{:S(2)}) collective-permute-start(bf16[1,32,256]{2,1,0:T(8,128)(2,1)S(1)} %fusion.115), channel_id=1, source_target_pairs={{0,64},{64,128},{128,192},{192,256},{256,320},{320,384},{384,448},... | collective-permute-start | bytes 49160 | tf_op jit(solution)/shard_map/ppermute | solution.py:25
  115.4 9.3 %collective-permute-start.33 = (bf16[1,32,256]{2,1,0:T(8,128)(2,1)S(1)}, bf16[1,32,256]{2,1,0:T(8,128)(2,1)S(1)}, u32[]{:S(2)}, u32[]{:S(2)}) collective-permute-start(bf16[1,32,256]{2,1,0:T(8,128)(2,1)S(1)} %fusion.122), channel_id=1, source_target_pairs={{64,0},{128,64},{192,128},{256,192},{320,256},{384,320},{448,384},... | collective-permute-start | bytes 49160 | tf_op jit(solution)/shard_map/ppermute | solution.py:25
  117.3 16.6 %collective-permute-start.13 = (bf16[1,32,256]{2,1,0:T(8,128)(2,1)S(1)}, bf16[1,32,256]{2,1,0:T(8,128)(2,1)S(1)}, u32[]{:S(2)}, u32[]{:S(2)}) collective-permute-start(bf16[1,32,256]{2,1,0:T(8,128)(2,1)S(1)} %collective-permute-done.12), channel_id=1, source_target_pairs={{0,1},{1,2},{2,3},{3,4},{4,5},{5,6},{6,7},{7,8},{8,9},{9,10},{10,1... | collective-permute-start | bytes 49160 | tf_op jit(solution)/shard_map/ppermute | solution.py:16
  122.8 11.1 %collective-permute-start.14 = (bf16[1,32,256]{2,1,0:T(8,128)(2,1)S(1)}, bf16[1,32,256]{2,1,0:T(8,128)(2,1)S(1)}, u32[]{:S(2)}, u32[]{:S(2)}) collective-permute-start(bf16[1,32,256]{2,1,0:T(8,128)(2,1)S(1)} %collective-permute-done.12), channel_id=1, source_target_pairs={{1,0},{2,1},{3,2},{4,3},{5,4},{6,5},{7,6},{8,7},{9,8},{10,9},{11,1... | collective-permute-start | bytes 49160 | tf_op jit(solution)/shard_map/ppermute | solution.py:17
  124.7 12.7 %collective-permute-start.34 = (bf16[1,32,256]{2,1,0:T(8,128)(2,1)S(1)}, bf16[1,32,256]{2,1,0:T(8,128)(2,1)S(1)}, u32[]{:S(2)}, u32[]{:S(2)}) collective-permute-start(bf16[1,32,256]{2,1,0:T(8,128)(2,1)S(1)} %collective-permute-done.33), channel_id=1, source_target_pairs={{0,1},{1,2},{2,3},{3,4},{4,5},{5,6},{6,7},{7,8},{8,9},{9,10},{10,1... | collective-permute-start | bytes 49160 | tf_op jit(solution)/shard_map/ppermute | solution.py:16
  132.0 9.0 %collective-permute-start.35 = (bf16[1,32,256]{2,1,0:T(8,128)(2,1)S(1)}, bf16[1,32,256]{2,1,0:T(8,128)(2,1)S(1)}, u32[]{:S(2)}, u32[]{:S(2)}) collective-permute-start(bf16[1,32,256]{2,1,0:T(8,128)(2,1)S(1)} %collective-permute-done.33), channel_id=1, source_target_pairs={{1,0},{2,1},{3,2},{4,3},{5,4},{6,5},{7,6},{8,7},{9,8},{10,9},{11,1... | collective-permute-start | bytes 49160 | tf_op jit(solution)/shard_map/ppermute | solution.py:17
  135.5 8.9 %collective-permute-start.15 = (bf16[1,32,256]{2,1,0:T(8,128)(2,1)S(1)}, bf16[1,32,256]{2,1,0:T(8,128)(2,1)S(1)}, u32[]{:S(2)}, u32[]{:S(2)}) collective-permute-start(bf16[1,32,256]{2,1,0:T(8,128)(2,1)S(1)} %fusion.116), channel_id=1, source_target_pairs={{0,64},{64,128},{128,192},{192,256},{256,320},{320,384},{384,448},... | collective-permute-start | bytes 49160 | tf_op jit(solution)/shard_map/ppermute | solution.py:25
  142.5 9.3 %collective-permute-start.36 = (bf16[1,32,256]{2,1,0:T(8,128)(2,1)S(1)}, bf16[1,32,256]{2,1,0:T(8,128)(2,1)S(1)}, u32[]{:S(2)}, u32[]{:S(2)}) collective-permute-start(bf16[1,32,256]{2,1,0:T(8,128)(2,1)S(1)} %fusion.123), channel_id=1, source_target_pairs={{64,0},{128,64},{192,128},{256,192},{320,256},{384,320},{448,384},... | collective-permute-start | bytes 49160 | tf_op jit(solution)/shard_map/ppermute | solution.py:25
  144.4 16.6 %collective-permute-start.16 = (bf16[1,32,256]{2,1,0:T(8,128)(2,1)S(1)}, bf16[1,32,256]{2,1,0:T(8,128)(2,1)S(1)}, u32[]{:S(2)}, u32[]{:S(2)}) collective-permute-start(bf16[1,32,256]{2,1,0:T(8,128)(2,1)S(1)} %collective-permute-done.15), channel_id=1, source_target_pairs={{0,1},{1,2},{2,3},{3,4},{4,5},{5,6},{6,7},{7,8},{8,9},{9,10},{10,1... | collective-permute-start | bytes 49160 | tf_op jit(solution)/shard_map/ppermute | solution.py:16
  149.9 11.1 %collective-permute-start.17 = (bf16[1,32,256]{2,1,0:T(8,128)(2,1)S(1)}, bf16[1,32,256]{2,1,0:T(8,128)(2,1)S(1)}, u32[]{:S(2)}, u32[]{:S(2)}) collective-permute-start(bf16[1,32,256]{2,1,0:T(8,128)(2,1)S(1)} %collective-permute-done.15), channel_id=1, source_target_pairs={{1,0},{2,1},{3,2},{4,3},{5,4},{6,5},{7,6},{8,7},{9,8},{10,9},{11,1... | collective-permute-start | bytes 49160 | tf_op jit(solution)/shard_map/ppermute | solution.py:17
  151.8 12.7 %collective-permute-start.37 = (bf16[1,32,256]{2,1,0:T(8,128)(2,1)S(1)}, bf16[1,32,256]{2,1,0:T(8,128)(2,1)S(1)}, u32[]{:S(2)}, u32[]{:S(2)}) collective-permute-start(bf16[1,32,256]{2,1,0:T(8,128)(2,1)S(1)} %collective-permute-done.36), channel_id=1, source_target_pairs={{0,1},{1,2},{2,3},{3,4},{4,5},{5,6},{6,7},{7,8},{8,9},{9,10},{10,1... | collective-permute-start | bytes 49160 | tf_op jit(solution)/shard_map/ppermute | solution.py:16
  159.1 9.0 %collective-permute-start.38 = (bf16[1,32,256]{2,1,0:T(8,128)(2,1)S(1)}, bf16[1,32,256]{2,1,0:T(8,128)(2,1)S(1)}, u32[]{:S(2)}, u32[]{:S(2)}) collective-permute-start(bf16[1,32,256]{2,1,0:T(8,128)(2,1)S(1)} %collective-permute-done.36), channel_id=1, source_target_pairs={{1,0},{2,1},{3,2},{4,3},{5,4},{6,5},{7,6},{8,7},{9,8},{10,9},{11,1... | collective-permute-start | bytes 49160 | tf_op jit(solution)/shard_map/ppermute | solution.py:17
  162.6 8.9 %collective-permute-start.18 = (bf16[1,32,256]{2,1,0:T(8,128)(2,1)S(1)}, bf16[1,32,256]{2,1,0:T(8,128)(2,1)S(1)}, u32[]{:S(2)}, u32[]{:S(2)}) collective-permute-start(bf16[1,32,256]{2,1,0:T(8,128)(2,1)S(1)} %fusion.117), channel_id=1, source_target_pairs={{0,64},{64,128},{128,192},{192,256},{256,320},{320,384},{384,448},... | collective-permute-start | bytes 49160 | tf_op jit(solution)/shard_map/ppermute | solution.py:25
  169.5 9.3 %collective-permute-start.39 = (bf16[1,32,256]{2,1,0:T(8,128)(2,1)S(1)}, bf16[1,32,256]{2,1,0:T(8,128)(2,1)S(1)}, u32[]{:S(2)}, u32[]{:S(2)}) collective-permute-start(bf16[1,32,256]{2,1,0:T(8,128)(2,1)S(1)} %fusion.124), channel_id=1, source_target_pairs={{64,0},{128,64},{192,128},{256,192},{320,256},{384,320},{448,384},... | collective-permute-start | bytes 49160 | tf_op jit(solution)/shard_map/ppermute | solution.py:25
  171.5 16.6 %collective-permute-start.19 = (bf16[1,32,256]{2,1,0:T(8,128)(2,1)S(1)}, bf16[1,32,256]{2,1,0:T(8,128)(2,1)S(1)}, u32[]{:S(2)}, u32[]{:S(2)}) collective-permute-start(bf16[1,32,256]{2,1,0:T(8,128)(2,1)S(1)} %collective-permute-done.18), channel_id=1, source_target_pairs={{0,1},{1,2},{2,3},{3,4},{4,5},{5,6},{6,7},{7,8},{8,9},{9,10},{10,1... | collective-permute-start | bytes 49160 | tf_op jit(solution)/shard_map/ppermute | solution.py:16
  177.0 11.1 %collective-permute-start.20 = (bf16[1,32,256]{2,1,0:T(8,128)(2,1)S(1)}, bf16[1,32,256]{2,1,0:T(8,128)(2,1)S(1)}, u32[]{:S(2)}, u32[]{:S(2)}) collective-permute-start(bf16[1,32,256]{2,1,0:T(8,128)(2,1)S(1)} %collective-permute-done.18), channel_id=1, source_target_pairs={{1,0},{2,1},{3,2},{4,3},{5,4},{6,5},{7,6},{8,7},{9,8},{10,9},{11,1... | collective-permute-start | bytes 49160 | tf_op jit(solution)/shard_map/ppermute | solution.py:17
  178.9 10.7 %collective-permute-start.40 = (bf16[1,32,256]{2,1,0:T(8,128)(2,1)S(1)}, bf16[1,32,256]{2,1,0:T(8,128)(2,1)S(1)}, u32[]{:S(2)}, u32[]{:S(2)}) collective-permute-start(bf16[1,32,256]{2,1,0:T(8,128)(2,1)S(1)} %collective-permute-done.39), channel_id=1, source_target_pairs={{0,1},{1,2},{2,3},{3,4},{4,5},{5,6},{6,7},{7,8},{8,9},{9,10},{10,1... | collective-permute-start | bytes 49160 | tf_op jit(solution)/shard_map/ppermute | solution.py:16
  186.1 9.0 %collective-permute-start.41 = (bf16[1,32,256]{2,1,0:T(8,128)(2,1)S(1)}, bf16[1,32,256]{2,1,0:T(8,128)(2,1)S(1)}, u32[]{:S(2)}, u32[]{:S(2)}) collective-permute-start(bf16[1,32,256]{2,1,0:T(8,128)(2,1)S(1)} %collective-permute-done.39), channel_id=1, source_target_pairs={{1,0},{2,1},{3,2},{4,3},{5,4},{6,5},{7,6},{8,7},{9,8},{10,9},{11,1... | collective-permute-start | bytes 49160 | tf_op jit(solution)/shard_map/ppermute | solution.py:17
where the time goes:
time: 199 us; the launch traced here: 197 us
  starting transfers between devices  144 us (72%)
  waiting for transfers between devices  26.7 us (13%)
  local copies, waits for them, and re-layouts  13 us (7%)
  matrix products  11 us (6%)
    ppermute x14, starting transfers between devices, padded(): before = lax.ppermute(last, axis, up)  88.2 us
    ppermute x14, starting transfers between devices, from_behind(): return lax.ppermute(block, axis, route)  28.6 us
    ppermute x14, starting transfers between devices, padded(): after = lax.ppermute(initial, axis, down)  26.9 us
    ppermute x14, waiting for transfers between devices, padded(): after = lax.ppermute(initial, axis, down)  26.6 us
    gather x14, local copies, waits for them, and re-layouts, apply_layer(): picked = jnp.take(blocks, cols - first, axis=1)  8.05 us
    dot_general x14, matrix products, apply_layer(): jnp.einsum('tij,stj->sti', tiles, picked, preferred_element_type=jnp.floa...  5.78 us
    dot_general x14, matrix products, apply_layer(): jnp.einsum('sti,tr->sri', product, onehot, precision=lax.Precision.HIGHEST)  5.23 us
  transfers between devices with their start and end apart: 42, of which 7 were waited for; matrix products, arithmetic and copies ran while one was open for 10% of the time, Pallas kernels for 0%

commit v1 on v0

v1 whole, which is shorter than its diff:
```python
import functools

import jax
import jax.numpy as jnp
from jax import lax
from jax.experimental import pallas as pl
from jax.experimental.pallas import tpu as pltpu
from jax.sharding import PartitionSpec as P

TILE = 128
MESH = pl.DeviceIdType.MESH
F32 = jnp.float32
BF16 = jnp.bfloat16


def kernel(
    rows_ref,
    cols_ref,
    order_ref,
    down_src,
    up_src,
    down_tiles,
    up_tiles,
    out_ref,
    src,
    own,
    tiles,
    band,
    recv,
    trace,
    src_sem,
    tile_sem,
    send_sem,
    recv_sem,
):
    layers, devices = lax.axis_size("layer"), lax.axis_size("rows")
    layer, k = lax.axis_index("layer"), lax.axis_index("rows")
    shots, width = own.shape[1], own.shape[2]
    local = width // TILE
    count = tiles.shape[1]

    src_copies = [
        pltpu.make_async_copy(ref.at[0], src.at[d], src_sem.at[d])
        for d, ref in enumerate((down_src, up_src))
    ]
    tile_copies = [
        pltpu.make_async_copy(ref.at[0], tiles.at[d], tile_sem.at[d])
        for d, ref in enumerate((down_tiles, up_tiles))
    ]
    for copy in src_copies + tile_copies:
        copy.start()

    barrier = pltpu.get_barrier_semaphore()

    def inside(dl, dk):
        return (
            (layer + dl >= 0) & (layer + dl < layers) & (k + dk >= 0) & (k + dk < devices)
        )

    for dl in (-1, 1):
        for dk in (-1, 1, 0):

            @pl.when(inside(dl, dk))
            def _():
                pl.semaphore_signal(
                    barrier, inc=1, device_id=(layer + dl, k + dk), device_id_type=MESH
                )

    @pl.when(k == 0)
    def _():
        for d in range(2):
            recv[d, 0] = jnp.zeros_like(recv[d, 0])

    @pl.when(k == devices - 1)
    def _():
        for d in range(2):
            recv[d, 2] = jnp.zeros_like(recv[d, 2])

    slot_of = lax.broadcasted_iota(jnp.int32, (shots, shots), 0)
    shot_of = lax.broadcasted_iota(jnp.int32, (shots, shots), 1)
    wanted = jnp.zeros((shots, shots), jnp.int32)
    for j in range(shots):
        wanted = jnp.where(slot_of == j, order_ref[j], wanted)
    pick = (shot_of == wanted).astype(F32).astype(BF16)
    for d in range(2):
        src_copies[d].wait()
        own[d] = jnp.dot(pick, src[d], preferred_element_type=F32).astype(BF16)

    def out_copy(d, dk):
        dl = 1 - 2 * d
        return pltpu.make_async_remote_copy(
            src_ref=trace.at[d],
            dst_ref=recv.at[d, 1 - dk],
            send_sem=send_sem.at[d, 1 - dk],
            recv_sem=recv_sem.at[d, 1 - dk],
            device_id=(layer + dl, k + dk),
            device_id_type=MESH,
        )

    def each_target(d, act):
        dl = 1 - 2 * d
        for dk in (-1, 1, 0):

            @pl.when(inside(dl, dk))
            def _():
                act(out_copy(d, dk))

    partners = ((layer > 0).astype(jnp.int32) + (layer < layers - 1).astype(jnp.int32)) * (
        1 + (k > 0).astype(jnp.int32) + (k < devices - 1).astype(jnp.int32)
    )
    pl.semaphore_wait(barrier, partners)

    for d, head in ((0, 0), (1, layers - 1)):

        @pl.when(layer == head)
        def _():
            trace[d] = own[d]
            each_target(d, lambda copy: copy.start())

    span = 3 * local
    place = []
    for t in range(count):
        row = rows_ref[0, t] - k * local
        col = cols_ref[0, t] - (k - 1) * local
        place.append(row * span + col)
    for d in range(2):
        tile_copies[d].wait()

    def build(step, carry):
        d, part = step // 8, step % 8
        lines = pl.ds(pl.multiple_of(part * 16, 16), 16)
        pieces = [tiles[d, t, lines, :].astype(F32) for t in range(count)]
        for r in range(local):
            for c in range(span):
                at = (d, c // local, pl.ds(pl.multiple_of(part * 16 + r * TILE, 16), 16))
                lanes = pl.ds((c % local) * TILE, TILE)
                if abs(c - local - r) > 2:
                    band[(*at, lanes)] = jnp.zeros((16, TILE), BF16)
                    continue
                total = jnp.zeros((16, TILE), F32)
                for t in range(count):
                    total = total + jnp.where(place[t] == r * span + c, pieces[t], 0.0)
                band[(*at, lanes)] = total.astype(BF16)
        return carry

    lax.fori_loop(0, 16, build, 0)

    for event in range(2):
        d = (layer // (layers // 2) + event) % 2
        head = d * (layers - 1)

        @pl.when(layer != head)
        def _():
            total = own[d].astype(F32)
            for b in (1, 0, 2):

                @pl.when((k - 1 + b >= 0) & (k - 1 + b < devices))
                def _():
                    pltpu.make_async_remote_copy(
                        src_ref=recv.at[d, b],
                        dst_ref=recv.at[d, b],
                        send_sem=send_sem.at[d, b],
                        recv_sem=recv_sem.at[d, b],
                        device_id=(layer, k),
                        device_id_type=MESH,
                    ).wait_recv()

                total = total + lax.dot_general(
                    recv[d, b], band[d, b], (((1,), (1,)), ((), ())), preferred_element_type=F32
                )
            trace[d] = total.astype(BF16)
            each_target(d, lambda copy: copy.start())

    out_ref[0] = (trace[0].astype(F32) + trace[1].astype(F32)).astype(BF16)
    for d in range(2):
        each_target(d, lambda copy: copy.wait_send())


def shards(down_sources, up_sources, down_tiles, up_tiles, tile_rows, tile_cols, shot_order):
    shots, width = down_sources.shape[1:]
    count = down_tiles.shape[1]
    anywhere = pl.BlockSpec(memory_space=pl.ANY)
    scalars = pl.BlockSpec(memory_space=pltpu.SMEM)
    return pl.pallas_call(
        kernel,
        name="sweeps",
        out_shape=jax.ShapeDtypeStruct(down_sources.shape, BF16),
        in_specs=[scalars] * 3 + [anywhere] * 4,
        out_specs=pl.BlockSpec(memory_space=pltpu.VMEM),
        scratch_shapes=[
            pltpu.VMEM((2, shots, width), BF16),
            pltpu.VMEM((2, shots, width), BF16),
            pltpu.VMEM((2, count, TILE, TILE), BF16),
            pltpu.VMEM((2, 3, width, width), BF16),
            pltpu.VMEM((2, 3, shots, width), BF16),
            pltpu.VMEM((2, shots, width), BF16),
            pltpu.SemaphoreType.DMA((2,)),
            pltpu.SemaphoreType.DMA((2,)),
            pltpu.SemaphoreType.DMA((2, 3)),
            pltpu.SemaphoreType.DMA((2, 3)),
        ],
        compiler_params=pltpu.CompilerParams(collective_id=0, has_side_effects=True),
    )(tile_rows, tile_cols, shot_order, down_sources, up_sources, down_tiles, up_tiles)


def solution(mesh):
    return jax.shard_map(
        shards,
        mesh=mesh,
        in_specs=(
            P("layer", None, "rows"),
            P("layer", None, "rows"),
            P("layer", "rows", None, None),
            P("layer", "rows", None, None),
            P("layer", "rows"),
            P("layer", "rows"),
            P(),
        ),
        out_specs=P("layer", None, "rows"),
        check_vma=False,
    )
```

time: 199 us -> 39.1 us (0.20)
  the two profiles are of different devices: /device:TPU:122 before, /device:TPU:384 now
where the time goes in v1:
time: 39.1 us; the launch traced here: 38.8 us
  Pallas kernels  37.4 us (96%)
  local copies, waits for them, and re-layouts  1.32 us (3%)
    pallas_call x1, Pallas kernels, shards(): pl.pallas_call(kernel, name='sweeps', out_shape=jax.ShapeDtypeStruct(down...  37.4 us
    unnamed x1, local copies, waits for them, and re-layouts  1.32 us

profile of v1, /device:TPU:384, one launch (start us, length us, event | category | flops | bytes accessed | tf_op | source)
XLA Modules:
  0.0 38.8 jit_solution(5000521359475489535)
XLA Ops:
  0.0 37.4 %sweeps.1 = bf16[1,32,256]{2,1,0:T(8,128)(2,1)} custom-call(s32[1,16]{1,0:T(1,128)} %rows_ref.1, s32[1,16]{1,0:T(1,128)} %cols_ref.1, s32[32]{0:T(128)} %order_ref.1, bf16[1,32,256]{2,1,0:T(8,128)(2,1)} %down_src.1, bf16[1,32,256]{2,1,0:T(8,128)(2,1)} %up_src.1, bf16[1,16,128,128]{3,2,1,0:T(8,128)(2,1)} %down_tiles.1, bf16[1,16,128,128]{3,2,1,0:T(8,128)(2,1)} %up_tiles.1), custom_call_target="tpu_custom_call" | custom-call | tf_op jit(solution)/shard_map/sweeps/pallas_call | solution.py:184
  37.5 1.3 %copy.9 = bf16[1,32,256]{2,1,0:T(8,128)(2,1)} copy(bf16[1,32,256]{2,1,0:T(8,128)(2,1)} %sweeps.1) | data formatting | bytes 32768

commit v2 on v0

v2 whole, which is shorter than its diff:
```python
import jax
import jax.numpy as jnp
from jax import lax
from jax.experimental import pallas as pl
from jax.experimental.pallas import tpu as pltpu
from jax.sharding import PartitionSpec as P

TILE = 128
MESH = pl.DeviceIdType.MESH
F32 = jnp.float32
BF16 = jnp.bfloat16
LEFT, HOME, RIGHT, SECOND, OTHER = range(5)
PART = 16


def band_rows(c, r):
    return 0 if c == 0 else TILE + 2 * TILE * (c - 1) + (r * TILE if c < 5 else 0)


def band_block(bands, slot, b):
    def tile(c, r):
        return bands[slot, pl.ds(band_rows(c, r), TILE), :]

    def line(r):
        pieces = [
            tile(c, r) if abs(c - 2 - r) <= 2 else jnp.zeros((TILE, TILE), BF16)
            for c in (2 * b, 2 * b + 1)
        ]
        return jnp.concatenate(pieces, axis=1)

    return jnp.concatenate([line(0), line(1)], axis=0)


def times(block, bands, slot, b):
    return lax.dot_general(
        block, band_block(bands, slot, b), (((1,), (1,)), ((), ())), preferred_element_type=F32
    )


def kernel(
    rows_hbm,
    cols_hbm,
    order_hbm,
    down_src,
    up_src,
    down_tiles,
    up_tiles,
    out_ref,
    rows_ref,
    cols_ref,
    order_ref,
    src,
    tiles,
    bands,
    terms,
    first,
    second,
    arrived,
    handed,
    scalar_sem,
    src_sem,
    tile_sem,
    band_send,
    band_recv,
    term_send,
    term_recv,
    source_send,
    source_recv,
    trace_send,
    trace_recv,
    hand_send,
    hand_recv,
    go,
):
    devices = lax.axis_size("rows")
    layer, k = lax.axis_index("layer"), lax.axis_index("rows")
    shots, width = src.shape[1], src.shape[2]
    local = width // TILE
    count = tiles.shape[1]

    x, core = layer // 2, layer % 2
    partner = 1 - core
    outer = (x == 0) | (x == 3)
    mine = jnp.where(outer, partner, core)
    X = jnp.where(mine == 0, x, 3 - x)
    ahead = 1 - 2 * mine
    mid = jnp.logical_not(outer)

    scalar_copies = [
        pltpu.make_async_copy(a, b, scalar_sem.at[i])
        for i, (a, b) in enumerate(
            ((rows_hbm, rows_ref), (cols_hbm, cols_ref), (order_hbm, order_ref))
        )
    ]
    src_copies = [
        pltpu.make_async_copy(ref.at[0], src.at[d], src_sem.at[d])
        for d, ref in enumerate((down_src, up_src))
    ]
    tile_copies = [
        pltpu.make_async_copy(ref.at[0], tiles.at[d], tile_sem.at[d])
        for d, ref in enumerate((down_tiles, up_tiles))
    ]
    for copy in scalar_copies + src_copies + tile_copies:
        copy.start()

    def exists(s):
        return (k + s >= 0) & (k + s < devices)

    def present(s):
        return exists(s).astype(jnp.int32)

    barrier = pltpu.get_barrier_semaphore()

    def greet(condition, x_to, core_to, s):
        @pl.when(condition & exists(s))
        def _():
            pl.semaphore_signal(
                barrier, inc=1, device_id=(x_to * 2 + core_to, k + s), device_id_type=MESH
            )

    for s in (-1, 1, 0):
        greet(True, x, partner if s == 0 else jnp.where(outer, partner, core), s)
    for s in (-2, 2, -1, 1, 0):
        greet(X >= 1, x - ahead, jnp.where(X == 1, 1 - mine, mine), s)

    for s in (-2, -1, 1, 2):

        @pl.when(jnp.logical_not(exists(s)))
        def _():
            arrived[2 + s] = jnp.zeros_like(arrived[2 + s])

    for s in (-1, 1):

        @pl.when(jnp.logical_not(exists(s)))
        def _():
            first[1 + s] = jnp.zeros_like(first[1 + s])
            terms[1 + s] = jnp.zeros_like(terms[1 + s])
            bands[1 + s] = jnp.zeros_like(bands[1 + s])

    for copy in scalar_copies:
        copy.wait()
    slot_of = lax.broadcasted_iota(jnp.int32, (shots, shots), 0)
    shot_of = lax.broadcasted_iota(jnp.int32, (shots, shots), 1)
    wanted = jnp.zeros((shots, shots), jnp.int32)
    for j in range(shots):
        wanted = jnp.where(slot_of == j, order_ref[j], wanted)
    pick = (shot_of == wanted).astype(F32).astype(BF16)
    for copy in src_copies:
        copy.wait()
    own = jnp.where(mid, HOME, SECOND)
    for sweep, slot in ((mine, own), (1 - mine, OTHER)):
        terms[slot] = jnp.dot(pick, src[sweep], preferred_element_type=F32).astype(BF16)

    place = []
    for t in range(count):
        row = rows_ref[t] - k * local
        col = cols_ref[t] - (k - 1) * local
        place.append(row * 3 * local + col)

    steps = TILE // PART

    def build(step, carry):
        other, part = step // steps, step % steps
        sweep = jnp.where(other == 0, mine, 1 - mine)
        slot = jnp.where(other == 0, own, OTHER)
        lines = pl.ds(pl.multiple_of(part * PART, PART), PART)
        pieces = [tiles[sweep, t, lines, :].astype(F32) for t in range(count)]
        for r in range(local):
            for c in range(r, r + 5):
                total = jnp.zeros((PART, TILE), F32)
                for t in range(count):
                    total = total + jnp.where(place[t] == r * 3 * local + c, pieces[t], 0.0)
                at = pl.ds(pl.multiple_of(band_rows(c, r) + part * PART, PART), PART)
                bands[slot, at, :] = total.astype(BF16)
        return carry

    def send(source, target, send_sem, recv_sem, x_to, core_to, s):
        return pltpu.make_async_remote_copy(
            src_ref=source,
            dst_ref=target,
            send_sem=send_sem,
            recv_sem=recv_sem,
            device_id=(x_to * 2 + core_to, k + s),
            device_id_type=MESH,
        )

    def await_recv(buffer, sem):
        pltpu.make_async_remote_copy(
            src_ref=buffer,
            dst_ref=buffer,
            send_sem=hand_send,
            recv_sem=sem,
            device_id=(layer, k),
            device_id_type=MESH,
        ).wait_recv()

    def when_all(condition, copies, act):
        for s, copy in copies:

            @pl.when(condition & exists(s))
            def _():
                act(copy(s))

    start = lambda copy: copy.start()
    wait_send = lambda copy: copy.wait_send()

    def near_term(s):
        return send(terms.at[HOME], terms.at[1 - s], term_send.at[1 + s], term_recv.at[1 - s], x, core, s)

    def near_band(s):
        return send(bands.at[HOME], bands.at[1 - s], band_send.at[1 + s], band_recv.at[1 - s], x, core, s)

    near = [(s, f) for f in (near_term, near_band) for s in (-1, 1)]

    def cross_slot(s):
        return jnp.where(mid, SECOND, 1 - s)

    def cross_term(s):
        to = cross_slot(s)
        return send(terms.at[OTHER], terms.at[to], term_send.at[4 + s], term_recv.at[to], x, partner, s)

    def cross_band(s):
        to = cross_slot(s)
        return send(bands.at[OTHER], bands.at[to], band_send.at[4 + s], band_recv.at[to], x, partner, s)

    cross_mid = [(0, cross_term), (0, cross_band)]
    cross_outer = [(s, f) for f in (cross_term, cross_band) for s in (-1, 1, 0)]

    def source(s):
        return send(
            terms.at[OTHER], first.at[1 - s], source_send.at[1 + s], source_recv.at[1 - s], x, partner, s
        )

    sources = [(s, source) for s in (-1, 1, 0)]

    def forward(s):
        core_to = jnp.where(X == 2, 1 - mine, mine)
        return send(
            second, arrived.at[2 - s], trace_send.at[2 + s], trace_recv.at[2 - s], x + ahead, core_to, s
        )

    forwards = [(s, forward) for s in (-2, 2, -1, 1, 0)]

    def hand(buffer):
        return send(buffer, handed, hand_send, hand_recv, x, partner, 0)

    @pl.when(X < 3)
    def _():
        for copy in tile_copies:
            copy.wait()
        lax.fori_loop(0, 2 * steps, build, 0)

    beside = present(-1) + present(0) + present(1)
    pl.semaphore_wait(
        barrier, beside + jnp.where(X < 3, beside + present(-2) + present(2), 0)
    )

    when_all(X == 3, sources, start)
    when_all(X == 1, near, start)
    when_all(mid, cross_mid, start)

    @pl.when(X == 3)
    def _():
        for copy in tile_copies:
            copy.wait()
        lax.fori_loop(0, steps, build, 0)

    when_all(X == 1, near, wait_send)

    @pl.when(X == 1)
    def _():
        pl.semaphore_signal(go, inc=1, device_id=(x * 2 + partner, k), device_id_type=MESH)

    @pl.when(X == 2)
    def _():
        pl.semaphore_wait(go, 1)

    when_all(X == 2, near, start)

    @pl.when(X == 0)
    def _():
        total = terms[SECOND].astype(F32)
        for b in (1, 0, 2):

            @pl.when(exists(b - 1))
            def _():
                await_recv(first.at[b], source_recv.at[b])

            total = total + times(first[b], bands, SECOND, b)
        second[...] = total.astype(BF16)

    when_all(X == 0, forwards, start)
    when_all(X == 0, cross_outer, start)

    @pl.when(X >= 1)
    def _():
        for slot in (HOME, LEFT, RIGHT, SECOND):
            from_far = mid if slot == SECOND else (X == 3) if slot == HOME else exists(slot - 1)

            @pl.when(from_far)
            def _():
                await_recv(terms.at[slot], term_recv.at[slot])
                await_recv(bands.at[slot], band_recv.at[slot])

        sums = [terms[t].astype(F32) for t in range(3)]
        total = terms[SECOND].astype(F32)
        for block, done in ((2, ()), (1, ()), (3, (1,)), (0, (0,)), (4, (2,))):

            @pl.when(exists(block - 2))
            def _():
                await_recv(arrived.at[block], trace_recv.at[block])

            for t in range(3):
                b = block - t
                if 0 <= b < 3:
                    sums[t] = sums[t] + times(arrived[block], bands, t, b)
            for t in done:
                value = sums[t].astype(BF16)
                first[t] = value
                if t == 1:

                    @pl.when(X == 3)
                    def _():
                        hand(first.at[1]).start()

                total = total + times(value, bands, SECOND, t)
        second[...] = total.astype(BF16)

    when_all(mid, forwards, start)

    @pl.when(mid)
    def _():
        hand(second).start()

    @pl.when(X == 3)
    def _():
        out_ref[0] = (second[...].astype(F32) + terms[OTHER].astype(F32)).astype(BF16)

    @pl.when(X < 3)
    def _():
        await_recv(handed, hand_recv)

    @pl.when(mid)
    def _():
        out_ref[0] = (first[1].astype(F32) + handed[...].astype(F32)).astype(BF16)

    @pl.when(X == 0)
    def _():
        out_ref[0] = (second[...].astype(F32) + handed[...].astype(F32)).astype(BF16)

    when_all(X == 3, sources, wait_send)
    when_all(X == 2, near, wait_send)
    when_all(mid, cross_mid, wait_send)
    when_all(X == 0, cross_outer, wait_send)
    when_all(X < 3, forwards, wait_send)

    @pl.when(X >= 1)
    def _():
        hand(second).wait_send()


def shards(down_sources, up_sources, down_tiles, up_tiles, tile_rows, tile_cols, shot_order):
    shots, width = down_sources.shape[1:]
    count = down_tiles.shape[1]
    anywhere = pl.BlockSpec(memory_space=pl.ANY)
    dma = pltpu.SemaphoreType.DMA
    return pl.pallas_call(
        kernel,
        name="sweeps",
        out_shape=jax.ShapeDtypeStruct(down_sources.shape, BF16),
        in_specs=[anywhere] * 7,
        out_specs=pl.BlockSpec(memory_space=pltpu.VMEM),
        scratch_shapes=[
            pltpu.SMEM((count,), jnp.int32),
            pltpu.SMEM((count,), jnp.int32),
            pltpu.SMEM(shot_order.shape, jnp.int32),
            pltpu.VMEM((2, shots, width), BF16),
            pltpu.VMEM((2, count, TILE, TILE), BF16),
            pltpu.VMEM((5, 10 * TILE, TILE), BF16),
            pltpu.VMEM((5, shots, width), BF16),
            pltpu.VMEM((3, shots, width), BF16),
            pltpu.VMEM((shots, width), BF16),
            pltpu.VMEM((5, shots, width), BF16),
            pltpu.VMEM((shots, width), BF16),
            dma((3,)),
            dma((2,)),
            dma((2,)),
            dma((6,)),
            dma((4,)),
            dma((6,)),
            dma((4,)),
            dma((3,)),
            dma((3,)),
            dma((5,)),
            dma((5,)),
            dma,
            dma,
            pltpu.SemaphoreType.REGULAR,
        ],
        compiler_params=pltpu.CompilerParams(collective_id=0, has_side_effects=True),
    )(tile_rows[0], tile_cols[0], shot_order, down_sources, up_sources, down_tiles, up_tiles)


def solution(mesh):
    return jax.shard_map(
        shards,
        mesh=mesh,
        in_specs=(
            P("layer", None, "rows"),
            P("layer", None, "rows"),
            P("layer", "rows", None, None),
            P("layer", "rows", None, None),
            P("layer", "rows"),
            P("layer", "rows"),
            P(),
        ),
        out_specs=P("layer", None, "rows"),
        check_vma=False,
    )
```

time: 199 us -> 29.7 us (0.15)
  the two profiles are of different devices: /device:TPU:122 before, /device:TPU:385 now
where the time goes in v2:
time: 29.7 us; the launch traced here: 29.5 us
  Pallas kernels  28.1 us (95%)
  local copies, waits for them, and re-layouts  1.32 us (4%)
    pallas_call x1, Pallas kernels, shards(): pl.pallas_call(kernel, name='sweeps', out_shape=jax.ShapeDtypeStruct(down...  28.1 us
    unnamed x1, local copies, waits for them, and re-layouts  1.32 us

profile of v2, /device:TPU:385, one launch (start us, length us, event | category | flops | bytes accessed | tf_op | source)
XLA Modules:
  0.0 29.5 jit_solution(6472335047370559076)
XLA Ops:
  0.0 28.1 %sweeps.1 = bf16[1,32,256]{2,1,0:T(8,128)(2,1)} custom-call(s32[16]{0:T(128)} %bitcast.2, s32[16]{0:T(128)} %bitcast.3, s32[32]{0:T(128)} %order_hbm.1, bf16[1,32,256]{2,1,0:T(8,128)(2,1)} %down_src.1, bf16[1,32,256]{2,1,0:T(8,128)(2,1)} %up_src.1, bf16[1,16,128,128]{3,2,1,0:T(8,128)(2,1)} %down_tiles.1, bf16[1,16,128,128]{3,2,1,0:T(8,128)(2,1)} %up_tiles.1), custom_call_target="tpu_custom_call" | custom-call | tf_op jit(solution)/shard_map/sweeps/pallas_call | solution.py:367
  28.1 1.3 %copy.9 = bf16[1,32,256]{2,1,0:T(8,128)(2,1)} copy(bf16[1,32,256]{2,1,0:T(8,128)(2,1)} %sweeps.1) | data formatting | bytes 32768

commit v3 on v2

v3 whole, which is shorter than its diff:
```python
import jax
import jax.numpy as jnp
from jax import lax
from jax.experimental import pallas as pl
from jax.experimental.pallas import tpu as pltpu
from jax.sharding import PartitionSpec as P

TILE = 128
MESH = pl.DeviceIdType.MESH
F32 = jnp.float32
BF16 = jnp.bfloat16
LEFT, HOME, RIGHT, SECOND = range(4)
SLOTS = 4
OUTGOING = 2 * SLOTS
PART = 16


def band_rows(c, r):
    return 0 if c == 0 else TILE + 2 * TILE * (c - 1) + (r * TILE if c < 5 else 0)


def band_block(bands, slot, b):
    def tile(c, r):
        return bands[slot, pl.ds(band_rows(c, r), TILE), :]

    def line(r):
        pieces = [
            tile(c, r) if abs(c - 2 - r) <= 2 else jnp.zeros((TILE, TILE), BF16)
            for c in (2 * b, 2 * b + 1)
        ]
        return jnp.concatenate(pieces, axis=1)

    return jnp.concatenate([line(0), line(1)], axis=0)


def times(block, bands, slot, b):
    return lax.dot_general(
        block, band_block(bands, slot, b), (((1,), (1,)), ((), ())), preferred_element_type=F32
    )


def kernel(
    rows_hbm,
    cols_hbm,
    order_hbm,
    down_src,
    up_src,
    down_tiles,
    up_tiles,
    out_ref,
    rows_ref,
    cols_ref,
    order_ref,
    src,
    tiles,
    bands,
    terms,
    first,
    centre,
    second,
    arrived,
    result,
    scalar_sem,
    src_sem,
    tile_sem,
    band_send,
    band_recv,
    term_send,
    term_recv,
    source_send,
    source_recv,
    trace_send,
    trace_recv,
    hand_send,
    hand_recv,
    go,
):
    devices = lax.axis_size("rows")
    layer, k = lax.axis_index("layer"), lax.axis_index("rows")
    shots, width = src.shape[1], src.shape[2]
    local = width // TILE
    count = tiles.shape[1]
    x, core = layer // 2, layer % 2
    partner = 1 - core
    early = x // 2

    def stage_of(d):
        return x + d * (3 - 2 * x)

    def layer_in(d):
        return core + d * (1 - 2 * core)

    def stage_core(d, at):
        return 1 - d * (at == 0).astype(jnp.int32)

    def event_of(d):
        return stage_of(d) // 2

    def is_source(d):
        return (stage_of(d) == 0) & (layer_in(d) == 0)

    def computes(d):
        return core == stage_core(d, x)

    def own_slot(d):
        inside = event_of(d) * SLOTS + jnp.where(layer_in(d) == 0, HOME, SECOND)
        return jnp.where(computes(d) & jnp.logical_not(is_source(d)), inside, OUTGOING + d)

    scalar_copies = [
        pltpu.make_async_copy(a, b, scalar_sem.at[i])
        for i, (a, b) in enumerate(
            ((rows_hbm, rows_ref), (cols_hbm, cols_ref), (order_hbm, order_ref))
        )
    ]
    src_copies = [
        pltpu.make_async_copy(ref.at[0], src.at[d], src_sem.at[d])
        for d, ref in enumerate((down_src, up_src))
    ]
    tile_copies = [
        pltpu.make_async_copy(ref.at[0], tiles.at[d], tile_sem.at[d])
        for d, ref in enumerate((down_tiles, up_tiles))
    ]

    def exists(s):
        return (k + s >= 0) & (k + s < devices)

    def present(s):
        return exists(s).astype(jnp.int32)

    barrier = pltpu.get_barrier_semaphore()

    def greet(condition, x_to, core_to, s):
        @pl.when(condition & exists(s))
        def _():
            pl.semaphore_signal(
                barrier, inc=1, device_id=(x_to * 2 + core_to, k + s), device_id_type=MESH
            )

    on_one = core == 1
    for s in (-1, 1):
        greet(on_one | (x == 0), x, partner, s)
        greet(on_one & (x >= 1), x, core, s)
    greet(True, x, partner, 0)
    for copy in scalar_copies + src_copies + tile_copies:
        copy.start()
    for s in (-2, 2, -1, 1, 0):
        greet(on_one & (x >= 1), x - 1, 1, s)
        greet((on_one & (x >= 1) & (x <= 2)) | (jnp.logical_not(on_one) & (x == 0)), x + 1, 1, s)

    for e in range(2):
        for s in (-2, -1, 1, 2):

            @pl.when(jnp.logical_not(exists(s)))
            def _():
                arrived[e, 2 + s] = jnp.zeros_like(arrived[e, 2 + s])

        for s in (-1, 1):

            @pl.when(jnp.logical_not(exists(s)))
            def _():
                at = e * SLOTS + 1 + s
                if e == 0:
                    first[1 + s] = jnp.zeros_like(first[1 + s])
                terms[at] = jnp.zeros_like(terms[at])
                bands[at] = jnp.zeros_like(bands[at])

    for copy in scalar_copies:
        copy.wait()
    slot_of = lax.broadcasted_iota(jnp.int32, (shots, shots), 0)
    shot_of = lax.broadcasted_iota(jnp.int32, (shots, shots), 1)
    wanted = jnp.zeros((shots, shots), jnp.int32)
    for j in range(shots):
        wanted = jnp.where(slot_of == j, order_ref[j], wanted)
    pick = (shot_of == wanted).astype(F32).astype(BF16)
    for copy in src_copies:
        copy.wait()
    for d in range(2):
        term = jnp.dot(pick, src[d], preferred_element_type=F32).astype(BF16)
        terms[own_slot(d)] = term

        @pl.when(is_source(d))
        def _():
            result[d] = term
            if d == 1:
                first[HOME] = term

    place = []
    for t in range(count):
        row = rows_ref[t] - k * local
        col = cols_ref[t] - (k - 1) * local
        place.append(row * 3 * local + col)

    steps = TILE // PART
    early_slot = jnp.where(early == 0, own_slot(0), own_slot(1))
    late_slot = jnp.where(early == 0, own_slot(1), own_slot(0))

    def build(step, carry):
        late, part = step // steps, step % steps
        sweep = (early + late) % 2
        slot = jnp.where(late == 0, early_slot, late_slot)
        lines = pl.ds(pl.multiple_of(part * PART, PART), PART)
        pieces = [tiles[sweep, t, lines, :].astype(F32) for t in range(count)]
        for r in range(local):
            for c in range(r, r + 5):
                total = jnp.zeros((PART, TILE), F32)
                for t in range(count):
                    total = total + jnp.where(place[t] == r * 3 * local + c, pieces[t], 0.0)
                at = pl.ds(pl.multiple_of(band_rows(c, r) + part * PART, PART), PART)
                bands[slot, at, :] = total.astype(BF16)
        return carry

    def build_from(start):
        for copy in tile_copies:
            copy.wait()
        lax.fori_loop(start, 2 * steps, build, 0)

    def send(source, target, send_sem, recv_sem, x_to, core_to, s):
        return pltpu.make_async_remote_copy(
            src_ref=source,
            dst_ref=target,
            send_sem=send_sem,
            recv_sem=recv_sem,
            device_id=(x_to * 2 + core_to, k + s),
            device_id_type=MESH,
        )

    def await_recv(buffer, sem):
        pltpu.make_async_remote_copy(
            src_ref=buffer,
            dst_ref=buffer,
            send_sem=hand_send.at[0],
            recv_sem=sem,
            device_id=(layer, k),
            device_id_type=MESH,
        ).wait_recv()

    start = lambda copy: copy.start()
    wait_send = lambda copy: copy.wait_send()

    def give(condition, d, act, seconds):
        for s in (0,) if seconds else (-1, 1, 0):
            remote = exists(s) if s else core != stage_core(d, x)
            kind = layer_in(d) == (1 if seconds else 0)

            @pl.when(condition & remote & kind & jnp.logical_not(is_source(d)))
            def _():
                at = own_slot(d)
                to = event_of(d) * SLOTS + (SECOND if seconds else 1 - s)
                for ref, ref_send, ref_recv in (
                    (terms, term_send, term_recv),
                    (bands, band_send, band_recv),
                ):
                    act(
                        send(
                            ref.at[at],
                            ref.at[to],
                            ref_send.at[d, 1 + s],
                            ref_recv.at[to],
                            x,
                            stage_core(d, x),
                            s,
                        )
                    )

    def sources(d, act):
        for s in (-1, 1, 0):
            remote = exists(s) if s else core != stage_core(d, x)

            @pl.when(is_source(d) & remote)
            def _():
                act(
                    send(
                        terms.at[OUTGOING + d],
                        first.at[1 - s],
                        source_send.at[1 + s],
                        source_recv.at[1 - s],
                        x,
                        stage_core(d, x),
                        s,
                    )
                )

    def forward(e, act):
        d = (early + e) % 2
        to = x + 1 - 2 * d
        for s in (-2, 2, -1, 1, 0):

            @pl.when(exists(s))
            def _():
                slot = (stage_of(d) + 1) // 2
                act(
                    send(
                        second.at[e],
                        arrived.at[slot, 2 - s],
                        trace_send.at[e, 2 + s],
                        trace_recv.at[slot, 2 - s],
                        to,
                        stage_core(d, to),
                        s,
                    )
                )

    def hand(e, d, from_second):
        return send(
            second.at[e] if from_second else centre.at[e],
            result.at[d],
            hand_send.at[e],
            hand_recv.at[d],
            x,
            partner,
            0,
        )

    origin = is_source(0) | is_source(1)

    @pl.when(jnp.logical_not(origin))
    def _():
        build_from(0)

    reach = present(-1) + present(0) + present(1)
    spread = reach + present(-2) + present(2)
    onward = (x <= 2).astype(jnp.int32) + (x >= 1).astype(jnp.int32)
    pl.semaphore_wait(barrier, reach + core * onward * spread)

    for d in range(2):
        sources(d, start)

    @pl.when(origin)
    def _():
        build_from(steps)

    for d in range(2):
        give(event_of(d) == 0, d, start, False)
    for d in range(2):
        give(True, d, start, True)

    between = (x >= 1) & (x <= 2)
    leads = between & (core == early)
    follows = between & (core != early)
    for d in range(2):
        give(leads & (event_of(d) == 0), d, wait_send, False)

    def let_go():
        pl.semaphore_signal(go, inc=1, device_id=(x * 2 + partner, k), device_id_type=MESH)

    @pl.when(leads)
    def _():
        let_go()

    @pl.when(follows)
    def _():
        pl.semaphore_wait(go, 1)

    for d in range(2):
        give(follows & (event_of(d) == 1), d, start, False)

    def event(e):
        d = (early + e) % 2
        X = stage_of(d)
        base = e * SLOTS
        ends_second = (d == 0) | (x == 0)

        def await_band(slot):
            here = exists(slot - 1)
            if slot == HOME:
                here = ends_second
            if slot == SECOND:
                here = jnp.logical_not(ends_second)

            @pl.when(here)
            def _():
                await_recv(terms.at[base + slot], term_recv.at[base + slot])
                await_recv(bands.at[base + slot], band_recv.at[base + slot])

        if e == 0:

            @pl.when(X == 0)
            def _():
                await_band(SECOND)
                total = terms[base + SECOND].astype(F32)
                for b in (1, 0, 2):

                    @pl.when(exists(b - 1) if b != 1 else d == 0)
                    def _():
                        await_recv(first.at[b], source_recv.at[b])

                    total = total + times(first[b], bands, base + SECOND, b)
                second[e] = total.astype(BF16)

        @pl.when(X >= 1)
        def _():
            for slot in (HOME, LEFT, RIGHT, SECOND):
                await_band(slot)
            sums = [terms[base + t].astype(F32) for t in range(3)]
            total = terms[base + SECOND].astype(F32)
            for block, done in ((2, ()), (1, ()), (3, (1,)), (0, (0,)), (4, (2,))):

                @pl.when(exists(block - 2))
                def _():
                    await_recv(arrived.at[e, block], trace_recv.at[e, block])

                for t in range(3):
                    b = block - t
                    if 0 <= b < 3:
                        sums[t] = sums[t] + times(arrived[e, block], bands, base + t, b)
                for t in done:
                    value = sums[t].astype(BF16)
                    if t == 1:
                        centre[e] = value

                        @pl.when(ends_second)
                        def _():
                            hand(e, d, False).start()

                    total = total + times(value, bands, base + SECOND, t)
            second[e] = total.astype(BF16)

        @pl.when(X < 3)
        def _():
            forward(e, start)

        @pl.when(ends_second)
        def _():
            result[d] = second[e]

        @pl.when(jnp.logical_not(ends_second))
        def _():
            hand(e, d, True).start()

            @pl.when(X >= 1)
            def _():
                result[d] = centre[e]

    @pl.when(on_one)
    def _():
        event(0)

    @pl.when(on_one & (x == 3))
    def _():
        let_go()

    @pl.when(jnp.logical_not(on_one) & (x == 3))
    def _():
        pl.semaphore_wait(go, 1)

    for d in range(2):
        give(((x == 0) | (x == 3)) & (event_of(d) == 1), d, start, False)

    late = on_one != (x == 0)

    @pl.when(late)
    def _():
        event(1)

    for d in range(2):

        @pl.when(jnp.logical_not(computes(d)) & jnp.logical_not(is_source(d)))
        def _():
            await_recv(result.at[d], hand_recv.at[d])

    out_ref[0] = (result[0].astype(F32) + result[1].astype(F32)).astype(BF16)

    for d in range(2):
        sources(d, wait_send)
        give(jnp.logical_not(leads & (event_of(d) == 0)), d, wait_send, False)
        give(True, d, wait_send, True)

    @pl.when(on_one)
    def _():
        forward(0, wait_send)

        @pl.when(x != 0)
        def _():
            hand(0, early, True).wait_send()

    @pl.when(late)
    def _():
        @pl.when(between)
        def _():
            forward(1, wait_send)

        hand(1, 1 - early, True).wait_send()


def shards(down_sources, up_sources, down_tiles, up_tiles, tile_rows, tile_cols, shot_order):
    shots, width = down_sources.shape[1:]
    count = down_tiles.shape[1]
    anywhere = pl.BlockSpec(memory_space=pl.ANY)
    dma = pltpu.SemaphoreType.DMA
    return pl.pallas_call(
        kernel,
        name="sweeps",
        out_shape=pltpu.VMEM(down_sources.shape, BF16),
        in_specs=[anywhere] * 7,
        out_specs=pl.BlockSpec(memory_space=pltpu.VMEM),
        scratch_shapes=[
            pltpu.SMEM((count,), jnp.int32),
            pltpu.SMEM((count,), jnp.int32),
            pltpu.SMEM(shot_order.shape, jnp.int32),
            pltpu.VMEM((2, shots, width), BF16),
            pltpu.VMEM((2, count, TILE, TILE), BF16),
            pltpu.VMEM((OUTGOING + 2, 10 * TILE, TILE), BF16),
            pltpu.VMEM((OUTGOING + 2, shots, width), BF16),
            pltpu.VMEM((3, shots, width), BF16),
            pltpu.VMEM((2, shots, width), BF16),
            pltpu.VMEM((2, shots, width), BF16),
            pltpu.VMEM((2, 5, shots, width), BF16),
            pltpu.VMEM((2, shots, width), BF16),
            dma((3,)),
            dma((2,)),
            dma((2,)),
            dma((2, 3)),
            dma((OUTGOING,)),
            dma((2, 3)),
            dma((OUTGOING,)),
            dma((3,)),
            dma((3,)),
            dma((2, 5)),
            dma((2, 5)),
            dma((2,)),
            dma((2,)),
            pltpu.SemaphoreType.REGULAR,
        ],
        compiler_params=pltpu.CompilerParams(collective_id=0, has_side_effects=True),
    )(tile_rows[0], tile_cols[0], shot_order, down_sources, up_sources, down_tiles, up_tiles)


def solution(mesh):
    return jax.shard_map(
        shards,
        mesh=mesh,
        in_specs=(
            P("layer", None, "rows"),
            P("layer", None, "rows"),
            P("layer", "rows", None, None),
            P("layer", "rows", None, None),
            P("layer", "rows"),
            P("layer", "rows"),
            P(),
        ),
        out_specs=P("layer", None, "rows"),
        check_vma=False,
    )
```

time: 29.7 us -> 28.2 us (0.949)
  local copies, waits for them, and re-layouts: 1.32 us -> 0.61 us
  Pallas kernels: 28.1 us -> 27.5 us
    unnamed x1, local copies, waits for them, and re-layouts: 1.32 us -> 0.61 us
    pallas_call x1, Pallas kernels: 28.1 us -> 27.5 us  [shards(): pl.pallas_call(kernel, name='sweeps', out_shape=pltpu.VMEM(down_sources.s...]
where the time goes in v3:
time: 28.2 us; the launch traced here: 28.1 us
  Pallas kernels  27.5 us (98%)
  local copies, waits for them, and re-layouts  0.61 us (2%)
    pallas_call x1, Pallas kernels, shards(): pl.pallas_call(kernel, name='sweeps', out_shape=pltpu.VMEM(down_sources.s...  27.5 us
    unnamed x1, local copies, waits for them, and re-layouts  0.61 us

profile of v3, /device:TPU:385, one launch (start us, length us, event | category | flops | bytes accessed | tf_op | source)
XLA Modules:
  0.0 28.1 jit_solution(7357326191425015313)
XLA Ops:
  0.0 27.5 %sweeps.1 = bf16[1,32,256]{2,1,0:T(8,128)(2,1)S(1)} custom-call(s32[16]{0:T(128)} %bitcast.2, s32[16]{0:T(128)} %bitcast.3, s32[32]{0:T(128)} %order_hbm.1, bf16[1,32,256]{2,1,0:T(8,128)(2,1)} %down_src.1, bf16[1,32,256]{2,1,0:T(8,128)(2,1)} %up_src.1, bf16[1,16,128,128]{3,2,1,0:T(8,128)(2,1)} %down_tiles.1, bf16[1,16,128,128]{3,2,1,0:T(8,128)(2,1)} %up_tiles.1), custom_call_target="tpu_custom_call" | custom-call | tf_op jit(solution)/shard_map/sweeps/pallas_call | solution.py:490
  27.5 0.6 %copy.9 = bf16[1,32,256]{2,1,0:T(8,128)(2,1)} copy(bf16[1,32,256]{2,1,0:T(8,128)(2,1)S(1)} %sweeps.1) | data formatting | bytes 32768

commit v4 on v3

--- a/solution.py
+++ b/solution.py
@@ -13,10 +13,14 @@
 SLOTS = 4
 OUTGOING = 2 * SLOTS
 PART = 16
+PLANE = 4
+
+
+REACH = 5 * TILE
 
 
 def band_rows(c, r):
-    return 0 if c == 0 else TILE + 2 * TILE * (c - 1) + (r * TILE if c < 5 else 0)
+    return r * REACH + (c - r) * TILE
 
 
 def band_block(bands, slot, b):
@@ -59,6 +63,8 @@
     centre,
     second,
     arrived,
+    beside,
+    products,
     result,
     scalar_sem,
     src_sem,
@@ -71,6 +77,8 @@
     source_recv,
     trace_send,
     trace_recv,
+    beside_send,
+    beside_recv,
     hand_send,
     hand_recv,
     go,
@@ -146,6 +154,9 @@
     for s in (-2, 2, -1, 1, 0):
         greet(on_one & (x >= 1), x - 1, 1, s)
         greet((on_one & (x >= 1) & (x <= 2)) | (jnp.logical_not(on_one) & (x == 0)), x + 1, 1, s)
+    tail = jnp.where(x == 0, on_one, jnp.logical_not(on_one) & (x == 3))
+    for s in (-1, 1, 0):
+        greet(tail, jnp.where(x == 0, x + 1, x - 1), 1, s)
 
     for e in range(2):
         for s in (-2, -1, 1, 2):
@@ -161,6 +172,7 @@
                 at = e * SLOTS + 1 + s
                 if e == 0:
                     first[1 + s] = jnp.zeros_like(first[1 + s])
+                    beside[1 + s] = jnp.zeros_like(beside[1 + s])
                 terms[at] = jnp.zeros_like(terms[at])
                 bands[at] = jnp.zeros_like(bands[at])
 
@@ -194,25 +206,22 @@
     early_slot = jnp.where(early == 0, own_slot(0), own_slot(1))
     late_slot = jnp.where(early == 0, own_slot(1), own_slot(0))
 
-    def build(step, carry):
-        late, part = step // steps, step % steps
+    def build(late, r):
         sweep = (early + late) % 2
-        slot = jnp.where(late == 0, early_slot, late_slot)
-        lines = pl.ds(pl.multiple_of(part * PART, PART), PART)
-        pieces = [tiles[sweep, t, lines, :].astype(F32) for t in range(count)]
-        for r in range(local):
+        slot = late_slot if late else early_slot
+
+        def step(part, carry):
+            lines = pl.ds(pl.multiple_of(part * PART, PART), PART)
+            pieces = [tiles[sweep, t, lines, :].astype(F32) for t in range(count)]
             for c in range(r, r + 5):
                 total = jnp.zeros((PART, TILE), F32)
                 for t in range(count):
                     total = total + jnp.where(place[t] == r * 3 * local + c, pieces[t], 0.0)
                 at = pl.ds(pl.multiple_of(band_rows(c, r) + part * PART, PART), PART)
                 bands[slot, at, :] = total.astype(BF16)
-        return carry
-
-    def build_from(start):
-        for copy in tile_copies:
-            copy.wait()
-        lax.fori_loop(start, 2 * steps, build, 0)
+            return carry
+
+        lax.fori_loop(0, steps, step, 0)
 
     def send(source, target, send_sem, recv_sem, x_to, core_to, s):
         return pltpu.make_async_remote_copy(
@@ -237,7 +246,7 @@
     start = lambda copy: copy.start()
     wait_send = lambda copy: copy.wait_send()
 
-    def give(condition, d, act, seconds):
+    def give(condition, d, act, seconds, terms_too=True, lines=(0, 1)):
         for s in (0,) if seconds else (-1, 1, 0):
             remote = exists(s) if s else core != stage_core(d, x)
             kind = layer_in(d) == (1 if seconds else 0)
@@ -246,19 +255,26 @@
             def _():
                 at = own_slot(d)
                 to = event_of(d) * SLOTS + (SECOND if seconds else 1 - s)
-                for ref, ref_send, ref_recv in (
-                    (terms, term_send, term_recv),
-                    (bands, band_send, band_recv),
-                ):
+                there = (x, stage_core(d, x), s)
+                if terms_too:
                     act(
                         send(
-                            ref.at[at],
-                            ref.at[to],
-                            ref_send.at[d, 1 + s],
-                            ref_recv.at[to],
-                            x,
-                            stage_core(d, x),
-                            s,
+                            terms.at[at],
+                            terms.at[to],
+                            term_send.at[d, 1 + s],
+                            term_recv.at[to],
+                            *there,
+                        )
+                    )
+                for r in lines:
+                    piece = pl.ds(r * REACH, REACH)
+                    act(
+                        send(
+                            bands.at[at, piece],
+                            bands.at[to, piece],
+                            band_send.at[d, 1 + s, r],
+                            band_recv.at[to, r],
+                            *there,
                         )
                     )
 
@@ -283,22 +299,42 @@
     def forward(e, act):
         d = (early + e) % 2
         to = x + 1 - 2 * d
-        for s in (-2, 2, -1, 1, 0):
-
-            @pl.when(exists(s))
-            def _():
-                slot = (stage_of(d) + 1) // 2
-                act(
-                    send(
-                        second.at[e],
-                        arrived.at[slot, 2 - s],
-                        trace_send.at[e, 2 + s],
-                        trace_recv.at[slot, 2 - s],
-                        to,
-                        stage_core(d, to),
-                        s,
-                    )
-                )
+        slot = (stage_of(d) + 1) // 2
+
+        def main(s):
+            return send(
+                second.at[e],
+                arrived.at[slot, 2 - s],
+                trace_send.at[e, 2 + s],
+                trace_recv.at[slot, 2 - s],
+                to,
+                stage_core(d, to),
+                s,
+            )
+
+        def extra(s):
+            return send(
+                second.at[e],
+                beside.at[1 - s],
+                beside_send.at[1 + s],
+                beside_recv.at[1 - s],
+                to,
+                1 - stage_core(d, to),
+                s,
+            )
+
+        for far in (True, False):
+            for copies, reached in ((main, (-1, 1, -2, 2, 0)), (extra, (-1, 1, 0))):
+                if copies is extra and e == 0:
+                    continue
+                for s in reached:
+                    if far and s == 0:
+                        continue
+                    side = (k % PLANE + s) // PLANE != 0
+
+                    @pl.when(exists(s) & (side if far else jnp.logical_not(side)))
+                    def _():
+                        act(copies(s))
 
     def hand(e, d, from_second):
         return send(
@@ -313,35 +349,47 @@
 
     origin = is_source(0) | is_source(1)
 
+    for copy in tile_copies:
+        copy.wait()
+
     @pl.when(jnp.logical_not(origin))
     def _():
-        build_from(0)
+        build(0, 0)
 
     reach = present(-1) + present(0) + present(1)
     spread = reach + present(-2) + present(2)
     onward = (x <= 2).astype(jnp.int32) + (x >= 1).astype(jnp.int32)
-    pl.semaphore_wait(barrier, reach + core * onward * spread)
+    between = (x >= 1) & (x <= 2)
+    pl.semaphore_wait(
+        barrier,
+        reach + core * (onward * spread + between.astype(jnp.int32) * reach),
+    )
 
     for d in range(2):
         sources(d, start)
-
-    @pl.when(origin)
-    def _():
-        build_from(steps)
-
-    for d in range(2):
-        give(event_of(d) == 0, d, start, False)
-    for d in range(2):
-        give(True, d, start, True)
-
-    between = (x >= 1) & (x <= 2)
+    for d in range(2):
+        for seconds in (False, True):
+            give(event_of(d) == 0, d, start, seconds, True, (0,))
+
+    @pl.when(jnp.logical_not(origin))
+    def _():
+        build(0, 1)
+
+    for d in range(2):
+        for seconds in (False, True):
+            give(event_of(d) == 0, d, start, seconds, False, (1,))
+    for r in range(2):
+        build(1, r)
+    for d in range(2):
+        give(event_of(d) == 1, d, start, True)
+
+    def let_go():
+        pl.semaphore_signal(go, inc=1, device_id=(x * 2 + partner, k), device_id_type=MESH)
+
     leads = between & (core == early)
     follows = between & (core != early)
     for d in range(2):
-        give(leads & (event_of(d) == 0), d, wait_send, False)
-
-    def let_go():
-        pl.semaphore_signal(go, inc=1, device_id=(x * 2 + partner, k), device_id_type=MESH)
+        give(leads & (event_of(d) == 0), d, wait_send, False, False, (0,))
 
     @pl.when(leads)
     def _():
@@ -370,7 +418,9 @@
             @pl.when(here)
             def _():
                 await_recv(terms.at[base + slot], term_recv.at[base + slot])
-                await_recv(bands.at[base + slot], band_recv.at[base + slot])
+                for r in range(2):
+                    piece = bands.at[base + slot, pl.ds(r * REACH, REACH)]
+                    await_recv(piece, band_recv.at[base + slot, r])
 
         if e == 0:
 
@@ -387,37 +437,80 @@
                     total = total + times(first[b], bands, base + SECOND, b)
                 second[e] = total.astype(BF16)
 
-        @pl.when(X >= 1)
-        def _():
+        def await_block(block):
+            @pl.when((k + block - 2 >= 0) & (k + block - 2 < devices))
+            def _():
+                await_recv(arrived.at[e, block], trace_recv.at[e, block])
+
+        if e == 0:
+
+            @pl.when(X >= 1)
+            def _():
+                for slot in (HOME, LEFT, RIGHT, SECOND):
+                    await_band(slot)
+                sums = [terms[base + t].astype(F32) for t in range(3)]
+                total = terms[base + SECOND].astype(F32)
+                for block, done in ((2, ()), (1, ()), (3, (1,)), (0, (0,)), (4, (2,))):
+                    await_block(block)
+                    for t in range(3):
+                        b = block - t
+                        if 0 <= b < 3:
+                            sums[t] = sums[t] + times(arrived[e, block], bands, base + t, b)
+                    for t in done:
+                        value = sums[t].astype(BF16)
+                        if t == 1:
+                            centre[e] = value
+                        total = total + times(value, bands, base + SECOND, t)
+                second[e] = total.astype(BF16)
+
+            forward(e, start)
+
+            @pl.when(X >= 1)
+            def _():
+                @pl.when(ends_second)
+                def _():
+                    hand(e, d, False).start()
+
+        else:
             for slot in (HOME, LEFT, RIGHT, SECOND):
                 await_band(slot)
-            sums = [terms[base + t].astype(F32) for t in range(3)]
             total = terms[base + SECOND].astype(F32)
-            for block, done in ((2, ()), (1, ()), (3, (1,)), (0, (0,)), (4, (2,))):
-
-                @pl.when(exists(block - 2))
-                def _():
-                    await_recv(arrived.at[e, block], trace_recv.at[e, block])
-
+            outer = [band_block(bands, base + SECOND, t) for t in range(3)]
+            for t in range(3):
+                total = total + times(terms[base + t], bands, base + SECOND, t)
+            for block in range(5):
+                product = None
                 for t in range(3):
                     b = block - t
                     if 0 <= b < 3:
-                        sums[t] = sums[t] + times(arrived[e, block], bands, base + t, b)
-                for t in done:
-                    value = sums[t].astype(BF16)
-                    if t == 1:
-                        centre[e] = value
-
-                        @pl.when(ends_second)
-                        def _():
-                            hand(e, d, False).start()
-
-                    total = total + times(value, bands, base + SECOND, t)
+                        part = jnp.dot(
+                            outer[t], band_block(bands, base + t, b), preferred_element_type=F32
+                        )
+                        product = part if product is None else product + part
+                products[block] = product.astype(BF16)
+            turn = 1 - 2 * (k % PLANE >= PLANE // 2).astype(jnp.int32)
+            for j in (0, 1, 2, -1, -2):
+                block = 2 + j * turn
+                await_block(block)
+                total = total + lax.dot_general(
+                    arrived[e, block],
+                    products[block],
+                    (((1,), (1,)), ((), ())),
+                    preferred_element_type=F32,
+                )
             second[e] = total.astype(BF16)
 
-        @pl.when(X < 3)
-        def _():
-            forward(e, start)
+            @pl.when(X < 3)
+            def _():
+                forward(e, start)
+                inner = terms[base + HOME].astype(F32)
+                for b in range(3):
+                    inner = inner + times(arrived[e, 1 + b], bands, base + HOME, b)
+                centre[e] = inner.astype(BF16)
+
+                @pl.when(ends_second)
+                def _():
+                    hand(e, d, False).start()
 
         @pl.when(ends_second)
         def _():
@@ -448,38 +541,60 @@
 
     late = on_one != (x == 0)
 
+    def finish():
+        for d in range(2):
+            sources(d, wait_send)
+            led = leads & (event_of(d) == 0)
+            give(led, d, wait_send, False, True, (1,))
+            give(jnp.logical_not(led), d, wait_send, False)
+            give(True, d, wait_send, True)
+
+        @pl.when(on_one)
+        def _():
+            forward(0, wait_send)
+
+            @pl.when(x != 0)
+            def _():
+                hand(0, early, True).wait_send()
+
+    @pl.when(jnp.logical_not(between))
+    def _():
+        finish()
+
     @pl.when(late)
     def _():
         event(1)
 
     for d in range(2):
-
-        @pl.when(jnp.logical_not(computes(d)) & jnp.logical_not(is_source(d)))
+        last = stage_of(d) == 3
+
+        @pl.when(tail & last)
+        def _():
+            at = OUTGOING + d
+            total = terms[at].astype(F32)
+            for b in (1, 0, 2):
+
+                @pl.when(exists(b - 1))
+                def _():
+                    await_recv(beside.at[b], beside_recv.at[b])
+
+                total = total + times(beside[b], bands, at, b)
+            result[d] = total.astype(BF16)
+
+        @pl.when(jnp.logical_not(computes(d) | is_source(d) | last))
         def _():
             await_recv(result.at[d], hand_recv.at[d])
 
     out_ref[0] = (result[0].astype(F32) + result[1].astype(F32)).astype(BF16)
 
-    for d in range(2):
-        sources(d, wait_send)
-        give(jnp.logical_not(leads & (event_of(d) == 0)), d, wait_send, False)
-        give(True, d, wait_send, True)
-
-    @pl.when(on_one)
-    def _():
-        forward(0, wait_send)
-
-        @pl.when(x != 0)
-        def _():
-            hand(0, early, True).wait_send()
-
-    @pl.when(late)
-    def _():
-        @pl.when(between)
+    @pl.when(between)
+    def _():
+        finish()
+
+        @pl.when(late)
         def _():
             forward(1, wait_send)
-
-        hand(1, 1 - early, True).wait_send()
+            hand(1, 1 - early, True).wait_send()
 
 
 def shards(down_sources, up_sources, down_tiles, up_tiles, tile_rows, tile_cols, shot_order):
@@ -505,18 +620,22 @@
             pltpu.VMEM((2, shots, width), BF16),
             pltpu.VMEM((2, shots, width), BF16),
             pltpu.VMEM((2, 5, shots, width), BF16),
+            pltpu.VMEM((3, shots, width), BF16),
+            pltpu.VMEM((5, width, width), BF16),
             pltpu.VMEM((2, shots, width), BF16),
             dma((3,)),
             dma((2,)),
             dma((2,)),
-            dma((2, 3)),
-            dma((OUTGOING,)),
+            dma((2, 3, 2)),
+            dma((OUTGOING, 2)),
             dma((2, 3)),
             dma((OUTGOING,)),
             dma((3,)),
             dma((3,)),
             dma((2, 5)),
             dma((2, 5)),
+            dma((3,)),
+            dma((3,)),
             dma((2,)),
             dma((2,)),
             pltpu.SemaphoreType.REGULAR,

time: 28.2 us -> 26.5 us (0.940)
  Pallas kernels: 27.5 us -> 25.8 us
    pallas_call x1, Pallas kernels: 27.5 us -> 25.8 us  [shards(): pl.pallas_call(kernel, name='sweeps', out_shape=pltpu.VMEM(down_sources.s...]
where the time goes in v4:
time: 26.5 us; the launch traced here: 26.4 us
  Pallas kernels  25.8 us (97%)
  local copies, waits for them, and re-layouts  0.61 us (2%)
    pallas_call x1, Pallas kernels, shards(): pl.pallas_call(kernel, name='sweeps', out_shape=pltpu.VMEM(down_sources.s...  25.8 us
    unnamed x1, local copies, waits for them, and re-layouts  0.61 us

profile of v4, /device:TPU:385, one launch (start us, length us, event | category | flops | bytes accessed | tf_op | source)
XLA Modules:
  0.0 26.4 jit_solution(2731758263632955833)
XLA Ops:
  0.0 25.8 %sweeps.1 = bf16[1,32,256]{2,1,0:T(8,128)(2,1)S(1)} custom-call(s32[16]{0:T(128)} %bitcast.2, s32[16]{0:T(128)} %bitcast.3, s32[32]{0:T(128)} %order_hbm.1, bf16[1,32,256]{2,1,0:T(8,128)(2,1)} %down_src.1, bf16[1,32,256]{2,1,0:T(8,128)(2,1)} %up_src.1, bf16[1,16,128,128]{3,2,1,0:T(8,128)(2,1)} %down_tiles.1, bf16[1,16,128,128]{3,2,1,0:T(8,128)(2,1)} %up_tiles.1), custom_call_target="tpu_custom_call" | custom-call | tf_op jit(solution)/shard_map/sweeps/pallas_call | solution.py:605
  25.8 0.6 %copy.9 = bf16[1,32,256]{2,1,0:T(8,128)(2,1)} copy(bf16[1,32,256]{2,1,0:T(8,128)(2,1)S(1)} %sweeps.1) | data formatting | bytes 32768

commit v5 on v4

--- a/solution.py
+++ b/solution.py
@@ -17,6 +17,7 @@
 
 
 REACH = 5 * TILE
+TERM = 64
 
 
 def band_rows(c, r):
@@ -71,17 +72,13 @@
     tile_sem,
     band_send,
     band_recv,
-    term_send,
-    term_recv,
-    source_send,
-    source_recv,
+    side_send,
     trace_send,
     trace_recv,
-    beside_send,
-    beside_recv,
     hand_send,
     hand_recv,
     go,
+    far,
 ):
     devices = lax.axis_size("rows")
     layer, k = lax.axis_index("layer"), lax.axis_index("rows")
@@ -121,11 +118,11 @@
         )
     ]
     src_copies = [
-        pltpu.make_async_copy(ref.at[0], src.at[d], src_sem.at[d])
+        pltpu.make_async_copy(ref.at[0], src.at[d], src_sem)
         for d, ref in enumerate((down_src, up_src))
     ]
     tile_copies = [
-        pltpu.make_async_copy(ref.at[0], tiles.at[d], tile_sem.at[d])
+        pltpu.make_async_copy(ref.at[0], tiles.at[d], tile_sem)
         for d, ref in enumerate((down_tiles, up_tiles))
     ]
 
@@ -151,12 +148,17 @@
     greet(True, x, partner, 0)
     for copy in scalar_copies + src_copies + tile_copies:
         copy.start()
+    def collector(x_to):
+        return (x_to <= 1).astype(jnp.int32)
+
     for s in (-2, 2, -1, 1, 0):
-        greet(on_one & (x >= 1), x - 1, 1, s)
-        greet((on_one & (x >= 1) & (x <= 2)) | (jnp.logical_not(on_one) & (x == 0)), x + 1, 1, s)
+        greet(on_one & (x >= 1), x - 1, collector(x - 1), s)
+        onto = (on_one & (x >= 1) & (x <= 2)) | (jnp.logical_not(on_one) & (x == 0))
+        greet(onto, x + 1, collector(x + 1), s)
     tail = jnp.where(x == 0, on_one, jnp.logical_not(on_one) & (x == 3))
     for s in (-1, 1, 0):
-        greet(tail, jnp.where(x == 0, x + 1, x - 1), 1, s)
+        to = jnp.where(x == 0, x + 1, x - 1)
+        greet(tail, to, collector(to), s)
 
     for e in range(2):
         for s in (-2, -1, 1, 2):
@@ -184,8 +186,7 @@
     for j in range(shots):
         wanted = jnp.where(slot_of == j, order_ref[j], wanted)
     pick = (shot_of == wanted).astype(F32).astype(BF16)
-    for copy in src_copies:
-        copy.wait()
+    pltpu.make_async_copy(src, src, src_sem).wait()
     for d in range(2):
         term = jnp.dot(pick, src[d], preferred_element_type=F32).astype(BF16)
         terms[own_slot(d)] = term
@@ -246,7 +247,7 @@
     start = lambda copy: copy.start()
     wait_send = lambda copy: copy.wait_send()
 
-    def give(condition, d, act, seconds, terms_too=True, lines=(0, 1)):
+    def give(condition, d, act, seconds, lines=(0, 1)):
         for s in (0,) if seconds else (-1, 1, 0):
             remote = exists(s) if s else core != stage_core(d, x)
             kind = layer_in(d) == (1 if seconds else 0)
@@ -255,28 +256,28 @@
             def _():
                 at = own_slot(d)
                 to = event_of(d) * SLOTS + (SECOND if seconds else 1 - s)
-                there = (x, stage_core(d, x), s)
-                if terms_too:
-                    act(
-                        send(
-                            terms.at[at],
-                            terms.at[to],
-                            term_send.at[d, 1 + s],
-                            term_recv.at[to],
-                            *there,
-                        )
+                lane = 3 if seconds else 1 + s
+
+                def part(source, target, r):
+                    return send(
+                        source,
+                        target,
+                        band_send.at[lane, r],
+                        band_recv.at[to, r],
+                        x,
+                        stage_core(d, x),
+                        s,
                     )
+
                 for r in lines:
+                    if act is wait_send:
+                        both = bands.at[at, pl.ds(0, REACH + r * TERM)]
+                        part(both, both, r).wait_send()
+                        continue
                     piece = pl.ds(r * REACH, REACH)
-                    act(
-                        send(
-                            bands.at[at, piece],
-                            bands.at[to, piece],
-                            band_send.at[d, 1 + s, r],
-                            band_recv.at[to, r],
-                            *there,
-                        )
-                    )
+                    act(part(bands.at[at, piece], bands.at[to, piece], r))
+                    if r == 1:
+                        act(part(terms.at[at], terms.at[to], r))
 
     def sources(d, act):
         for s in (-1, 1, 0):
@@ -288,8 +289,8 @@
                     send(
                         terms.at[OUTGOING + d],
                         first.at[1 - s],
-                        source_send.at[1 + s],
-                        source_recv.at[1 - s],
+                        side_send.at[1 + s],
+                        trace_recv.at[0, 2 - s],
                         x,
                         stage_core(d, x),
                         s,
@@ -305,7 +306,7 @@
             return send(
                 second.at[e],
                 arrived.at[slot, 2 - s],
-                trace_send.at[e, 2 + s],
+                trace_send.at[e],
                 trace_recv.at[slot, 2 - s],
                 to,
                 stage_core(d, to),
@@ -316,23 +317,40 @@
             return send(
                 second.at[e],
                 beside.at[1 - s],
-                beside_send.at[1 + s],
-                beside_recv.at[1 - s],
+                side_send.at[1 + s],
+                trace_recv.at[1, 2 - s],
                 to,
                 1 - stage_core(d, to),
                 s,
             )
 
-        for far in (True, False):
+        if act is wait_send:
+            for n in (3, 4, 5):
+
+                @pl.when(spread == n)
+                def _():
+                    blocks = arrived.at[0, pl.ds(0, n)]
+                    send(blocks, blocks, trace_send.at[e], trace_recv.at[0, 0], x, partner, 0).wait_send()
+
+            if e == 1:
+                for s in (-1, 1, 0):
+
+                    @pl.when(exists(s))
+                    def _():
+                        extra(s).wait_send()
+
+            return
+
+        for crossing in (True, False):
             for copies, reached in ((main, (-1, 1, -2, 2, 0)), (extra, (-1, 1, 0))):
                 if copies is extra and e == 0:
                     continue
                 for s in reached:
-                    if far and s == 0:
+                    if crossing and s == 0:
                         continue
                     side = (k % PLANE + s) // PLANE != 0
 
-                    @pl.when(exists(s) & (side if far else jnp.logical_not(side)))
+                    @pl.when(exists(s) & (side if crossing else jnp.logical_not(side)))
                     def _():
                         act(copies(s))
 
@@ -349,35 +367,46 @@
 
     origin = is_source(0) | is_source(1)
 
-    for copy in tile_copies:
-        copy.wait()
+    pltpu.make_async_copy(tiles, tiles, tile_sem).wait()
 
     @pl.when(jnp.logical_not(origin))
     def _():
         build(0, 0)
+
+    patient = jnp.logical_not(on_one) & (x >= 2)
+
+    @pl.when(patient)
+    def _():
+        build(0, 1)
 
     reach = present(-1) + present(0) + present(1)
     spread = reach + present(-2) + present(2)
     onward = (x <= 2).astype(jnp.int32) + (x >= 1).astype(jnp.int32)
     between = (x >= 1) & (x <= 2)
+    collects = core == collector(x)
     pl.semaphore_wait(
         barrier,
-        reach + core * (onward * spread + between.astype(jnp.int32) * reach),
+        reach
+        + collects.astype(jnp.int32) * (onward * spread + between.astype(jnp.int32) * reach),
     )
 
+    @pl.when(collects & (x >= 2))
+    def _():
+        pl.semaphore_signal(far, inc=1, device_id=(x * 2 + partner, k), device_id_type=MESH)
+
     for d in range(2):
         sources(d, start)
     for d in range(2):
         for seconds in (False, True):
-            give(event_of(d) == 0, d, start, seconds, True, (0,))
-
-    @pl.when(jnp.logical_not(origin))
+            give(event_of(d) == 0, d, start, seconds, (0,))
+
+    @pl.when(jnp.logical_not(origin | patient))
     def _():
         build(0, 1)
 
     for d in range(2):
         for seconds in (False, True):
-            give(event_of(d) == 0, d, start, seconds, False, (1,))
+            give(event_of(d) == 0, d, start, seconds, (1,))
     for r in range(2):
         build(1, r)
     for d in range(2):
@@ -389,7 +418,7 @@
     leads = between & (core == early)
     follows = between & (core != early)
     for d in range(2):
-        give(leads & (event_of(d) == 0), d, wait_send, False, False, (0,))
+        give(leads & (event_of(d) == 0), d, wait_send, False, (0,))
 
     @pl.when(leads)
     def _():
@@ -417,9 +446,8 @@
 
             @pl.when(here)
             def _():
-                await_recv(terms.at[base + slot], term_recv.at[base + slot])
                 for r in range(2):
-                    piece = bands.at[base + slot, pl.ds(r * REACH, REACH)]
+                    piece = bands.at[base + slot, pl.ds(0, REACH + r * TERM)]
                     await_recv(piece, band_recv.at[base + slot, r])
 
         if e == 0:
@@ -432,7 +460,7 @@
 
                     @pl.when(exists(b - 1) if b != 1 else d == 0)
                     def _():
-                        await_recv(first.at[b], source_recv.at[b])
+                        await_recv(first.at[b], trace_recv.at[0, 1 + b])
 
                     total = total + times(first[b], bands, base + SECOND, b)
                 second[e] = total.astype(BF16)
@@ -462,6 +490,10 @@
                             centre[e] = value
                         total = total + times(value, bands, base + SECOND, t)
                 second[e] = total.astype(BF16)
+
+            @pl.when(x >= 2)
+            def _():
+                pl.semaphore_wait(far, 1)
 
             forward(e, start)
 
@@ -545,7 +577,7 @@
         for d in range(2):
             sources(d, wait_send)
             led = leads & (event_of(d) == 0)
-            give(led, d, wait_send, False, True, (1,))
+            give(led, d, wait_send, False, (1,))
             give(jnp.logical_not(led), d, wait_send, False)
             give(True, d, wait_send, True)
 
@@ -576,7 +608,7 @@
 
                 @pl.when(exists(b - 1))
                 def _():
-                    await_recv(beside.at[b], beside_recv.at[b])
+                    await_recv(beside.at[b], trace_recv.at[1, 1 + b])
 
                 total = total + times(beside[b], bands, at, b)
             result[d] = total.astype(BF16)
@@ -624,20 +656,16 @@
             pltpu.VMEM((5, width, width), BF16),
             pltpu.VMEM((2, shots, width), BF16),
             dma((3,)),
+            dma,
+            dma,
+            dma((4, 2)),
+            dma((OUTGOING, 2)),
+            dma((3,)),
+            dma((2,)),
+            dma((2, 5)),
             dma((2,)),
             dma((2,)),
-            dma((2, 3, 2)),
-            dma((OUTGOING, 2)),
-            dma((2, 3)),
-            dma((OUTGOING,)),
-            dma((3,)),
-            dma((3,)),
-            dma((2, 5)),
-            dma((2, 5)),
-            dma((3,)),
-            dma((3,)),
-            dma((2,)),
-            dma((2,)),
+            pltpu.SemaphoreType.REGULAR,
             pltpu.SemaphoreType.REGULAR,
         ],
         compiler_params=pltpu.CompilerParams(collective_id=0, has_side_effects=True),

time: 26.5 us -> 25.7 us (0.970)
  Pallas kernels: 25.8 us -> 24.9 us
    pallas_call x1, Pallas kernels: 25.8 us -> 24.9 us  [shards(): pl.pallas_call(kernel, name='sweeps', out_shape=pltpu.VMEM(down_sources.s...]
where the time goes in v5:
time: 25.7 us; the launch traced here: 25.6 us
  Pallas kernels  24.9 us (97%)
  local copies, waits for them, and re-layouts  0.61 us (2%)
    pallas_call x1, Pallas kernels, shards(): pl.pallas_call(kernel, name='sweeps', out_shape=pltpu.VMEM(down_sources.s...  24.9 us
    unnamed x1, local copies, waits for them, and re-layouts  0.61 us

profile of v5, /device:TPU:385, one launch (start us, length us, event | category | flops | bytes accessed | tf_op | source)
XLA Modules:
  0.0 25.6 jit_solution(6330679474979518765)
XLA Ops:
  0.0 24.9 %sweeps.1 = bf16[1,32,256]{2,1,0:T(8,128)(2,1)S(1)} custom-call(s32[16]{0:T(128)} %bitcast.2, s32[16]{0:T(128)} %bitcast.3, s32[32]{0:T(128)} %order_hbm.1, bf16[1,32,256]{2,1,0:T(8,128)(2,1)} %down_src.1, bf16[1,32,256]{2,1,0:T(8,128)(2,1)} %up_src.1, bf16[1,16,128,128]{3,2,1,0:T(8,128)(2,1)} %down_tiles.1, bf16[1,16,128,128]{3,2,1,0:T(8,128)(2,1)} %up_tiles.1), custom_call_target="tpu_custom_call" | custom-call | tf_op jit(solution)/shard_map/sweeps/pallas_call | solution.py:637
  24.9 0.6 %copy.9 = bf16[1,32,256]{2,1,0:T(8,128)(2,1)} copy(bf16[1,32,256]{2,1,0:T(8,128)(2,1)S(1)} %sweeps.1) | data formatting | bytes 32768

commit v6 on v5

--- a/solution.py
+++ b/solution.py
@@ -38,10 +38,14 @@
     return jnp.concatenate([line(0), line(1)], axis=0)
 
 
+def times_all(block, matrix):
+    return lax.dot_general(
+        block, matrix, (((1,), (1,)), ((), ())), preferred_element_type=F32
+    )
+
+
 def times(block, bands, slot, b):
-    return lax.dot_general(
-        block, band_block(bands, slot, b), (((1,), (1,)), ((), ())), preferred_element_type=F32
-    )
+    return times_all(block, band_block(bands, slot, b))
 
 
 def kernel(
@@ -65,6 +69,8 @@
     second,
     arrived,
     beside,
+    outer,
+    sums,
     products,
     result,
     scalar_sem,
@@ -247,10 +253,15 @@
     start = lambda copy: copy.start()
     wait_send = lambda copy: copy.wait_send()
 
-    def give(condition, d, act, seconds, lines=(0, 1)):
+    def leaves_plane(s):
+        return (k % PLANE + s) // PLANE != 0
+
+    def give(condition, d, act, seconds, lines=(0, 1), crossing=None):
         for s in (0,) if seconds else (-1, 1, 0):
             remote = exists(s) if s else core != stage_core(d, x)
             kind = layer_in(d) == (1 if seconds else 0)
+            if crossing is not None:
+                kind = kind & (leaves_plane(s) == crossing)
 
             @pl.when(condition & remote & kind & jnp.logical_not(is_source(d)))
             def _():
@@ -348,7 +359,7 @@
                 for s in reached:
                     if crossing and s == 0:
                         continue
-                    side = (k % PLANE + s) // PLANE != 0
+                    side = leaves_plane(s)
 
                     @pl.when(exists(s) & (side if crossing else jnp.logical_not(side)))
                     def _():
@@ -439,9 +450,9 @@
 
         def await_band(slot):
             here = exists(slot - 1)
-            if slot == HOME:
+            if slot is HOME:
                 here = ends_second
-            if slot == SECOND:
+            if slot is SECOND:
                 here = jnp.logical_not(ends_second)
 
             @pl.when(here)
@@ -470,79 +481,51 @@
             def _():
                 await_recv(arrived.at[e, block], trace_recv.at[e, block])
 
-        if e == 0:
-
-            @pl.when(X >= 1)
-            def _():
-                for slot in (HOME, LEFT, RIGHT, SECOND):
-                    await_band(slot)
-                sums = [terms[base + t].astype(F32) for t in range(3)]
-                total = terms[base + SECOND].astype(F32)
-                for block, done in ((2, ()), (1, ()), (3, (1,)), (0, (0,)), (4, (2,))):
-                    await_block(block)
-                    for t in range(3):
-                        b = block - t
-                        if 0 <= b < 3:
-                            sums[t] = sums[t] + times(arrived[e, block], bands, base + t, b)
-                    for t in done:
-                        value = sums[t].astype(BF16)
-                        if t == 1:
-                            centre[e] = value
-                        total = total + times(value, bands, base + SECOND, t)
-                second[e] = total.astype(BF16)
-
-            @pl.when(x >= 2)
-            def _():
-                pl.semaphore_wait(far, 1)
-
-            forward(e, start)
-
-            @pl.when(X >= 1)
-            def _():
-                @pl.when(ends_second)
-                def _():
-                    hand(e, d, False).start()
-
-        else:
-            for slot in (HOME, LEFT, RIGHT, SECOND):
-                await_band(slot)
+        @pl.when(X >= 1)
+        def _():
+            turn = 1 - 2 * (k % PLANE >= PLANE // 2).astype(jnp.int32)
+            await_band(SECOND)
+            for t in range(3):
+                outer[t] = band_block(bands, base + SECOND, t)
+            for block in (0, 4):
+                sums[block] = jnp.zeros_like(sums[block])
             total = terms[base + SECOND].astype(F32)
-            outer = [band_block(bands, base + SECOND, t) for t in range(3)]
-            for t in range(3):
-                total = total + times(terms[base + t], bands, base + SECOND, t)
+            for t in (HOME, 1 + turn, 1 - turn):
+                await_band(t)
+                total = total + times_all(terms[base + t], outer[t])
+                for b in range(3):
+                    product = jnp.dot(
+                        outer[t], band_block(bands, base + t, b), preferred_element_type=F32
+                    )
+                    sums[t + b] = product if t is HOME else sums[t + b] + product
             for block in range(5):
-                product = None
-                for t in range(3):
-                    b = block - t
-                    if 0 <= b < 3:
-                        part = jnp.dot(
-                            outer[t], band_block(bands, base + t, b), preferred_element_type=F32
-                        )
-                        product = part if product is None else product + part
-                products[block] = product.astype(BF16)
-            turn = 1 - 2 * (k % PLANE >= PLANE // 2).astype(jnp.int32)
+                products[block] = sums[block].astype(BF16)
             for j in (0, 1, 2, -1, -2):
                 block = 2 + j * turn
                 await_block(block)
-                total = total + lax.dot_general(
-                    arrived[e, block],
-                    products[block],
-                    (((1,), (1,)), ((), ())),
-                    preferred_element_type=F32,
-                )
+                total = total + times_all(arrived[e, block], products[block])
             second[e] = total.astype(BF16)
 
-            @pl.when(X < 3)
-            def _():
-                forward(e, start)
-                inner = terms[base + HOME].astype(F32)
-                for b in range(3):
-                    inner = inner + times(arrived[e, 1 + b], bands, base + HOME, b)
-                centre[e] = inner.astype(BF16)
-
-                @pl.when(ends_second)
-                def _():
-                    hand(e, d, False).start()
+        if e == 0:
+
+            @pl.when(x >= 2)
+            def _():
+                pl.semaphore_wait(far, 1)
+
+        @pl.when(X < 3)
+        def _():
+            forward(e, start)
+
+        @pl.when((X == 1) | (X == 2))
+        def _():
+            inner = terms[base + HOME].astype(F32)
+            for b in range(3):
+                inner = inner + times(arrived[e, 1 + b], bands, base + HOME, b)
+            centre[e] = inner.astype(BF16)
+
+            @pl.when(ends_second)
+            def _():
+                hand(e, d, False).start()
 
         @pl.when(ends_second)
         def _():
@@ -653,6 +636,8 @@
             pltpu.VMEM((2, shots, width), BF16),
             pltpu.VMEM((2, 5, shots, width), BF16),
             pltpu.VMEM((3, shots, width), BF16),
+            pltpu.VMEM((3, width, width), BF16),
+            pltpu.VMEM((5, width, width), F32),
             pltpu.VMEM((5, width, width), BF16),
             pltpu.VMEM((2, shots, width), BF16),
             dma((3,)),

time: 25.7 us -> 25.2 us (0.981)
  Pallas kernels: 24.9 us -> 24.5 us
    pallas_call x1, Pallas kernels: 24.9 us -> 24.5 us  [shards(): pl.pallas_call(kernel, name='sweeps', out_shape=pltpu.VMEM(down_sources.s...]
where the time goes in v6:
time: 25.2 us; the launch traced here: 25.1 us
  Pallas kernels  24.5 us (97%)
  local copies, waits for them, and re-layouts  0.61 us (2%)
    pallas_call x1, Pallas kernels, shards(): pl.pallas_call(kernel, name='sweeps', out_shape=pltpu.VMEM(down_sources.s...  24.5 us
    unnamed x1, local copies, waits for them, and re-layouts  0.61 us

profile of v6, /device:TPU:385, one launch (start us, length us, event | category | flops | bytes accessed | tf_op | source)
XLA Modules:
  0.0 25.1 jit_solution(7408238663662383468)
XLA Ops:
  0.0 24.5 %sweeps.1 = bf16[1,32,256]{2,1,0:T(8,128)(2,1)S(1)} custom-call(s32[16]{0:T(128)} %bitcast.2, s32[16]{0:T(128)} %bitcast.3, s32[32]{0:T(128)} %order_hbm.1, bf16[1,32,256]{2,1,0:T(8,128)(2,1)} %down_src.1, bf16[1,32,256]{2,1,0:T(8,128)(2,1)} %up_src.1, bf16[1,16,128,128]{3,2,1,0:T(8,128)(2,1)} %down_tiles.1, bf16[1,16,128,128]{3,2,1,0:T(8,128)(2,1)} %up_tiles.1), custom_call_target="tpu_custom_call" | custom-call | tf_op jit(solution)/shard_map/sweeps/pallas_call | solution.py:620
  24.5 0.6 %copy.9 = bf16[1,32,256]{2,1,0:T(8,128)(2,1)} copy(bf16[1,32,256]{2,1,0:T(8,128)(2,1)S(1)} %sweeps.1) | data formatting | bytes 32768

commit v7 on v6

--- a/solution.py
+++ b/solution.py
@@ -84,7 +84,6 @@
     hand_send,
     hand_recv,
     go,
-    far,
 ):
     devices = lax.axis_size("rows")
     layer, k = lax.axis_index("layer"), lax.axis_index("rows")
@@ -244,71 +243,95 @@
         pltpu.make_async_remote_copy(
             src_ref=buffer,
             dst_ref=buffer,
-            send_sem=hand_send.at[0],
+            send_sem=hand_send,
             recv_sem=sem,
             device_id=(layer, k),
             device_id_type=MESH,
         ).wait_recv()
 
-    start = lambda copy: copy.start()
-    wait_send = lambda copy: copy.wait_send()
+    turn = 1 - 2 * (k % PLANE >= PLANE // 2).astype(jnp.int32)
 
     def leaves_plane(s):
         return (k % PLANE + s) // PLANE != 0
 
-    def give(condition, d, act, seconds, lines=(0, 1), crossing=None):
+    def give(condition, d, seconds, lines=(0, 1)):
         for s in (0,) if seconds else (-1, 1, 0):
             remote = exists(s) if s else core != stage_core(d, x)
             kind = layer_in(d) == (1 if seconds else 0)
-            if crossing is not None:
-                kind = kind & (leaves_plane(s) == crossing)
 
             @pl.when(condition & remote & kind & jnp.logical_not(is_source(d)))
             def _():
                 at = own_slot(d)
                 to = event_of(d) * SLOTS + (SECOND if seconds else 1 - s)
-                lane = 3 if seconds else 1 + s
 
                 def part(source, target, r):
                     return send(
                         source,
                         target,
-                        band_send.at[lane, r],
-                        band_recv.at[to, r],
+                        band_send.at[2 if seconds else r],
+                        band_recv.at[to],
                         x,
                         stage_core(d, x),
                         s,
                     )
 
                 for r in lines:
-                    if act is wait_send:
-                        both = bands.at[at, pl.ds(0, REACH + r * TERM)]
-                        part(both, both, r).wait_send()
-                        continue
                     piece = pl.ds(r * REACH, REACH)
-                    act(part(bands.at[at, piece], bands.at[to, piece], r))
+                    part(bands.at[at, piece], bands.at[to, piece], r).start()
                     if r == 1:
-                        act(part(terms.at[at], terms.at[to], r))
-
-    def sources(d, act):
+                        part(terms.at[at], terms.at[to], r).start()
+
+    def await_sent(condition, buffer, sem):
+        @pl.when(condition)
+        def _():
+            send(buffer, buffer, sem, band_recv.at[0], x, partner, 0).wait_send()
+
+    def await_given(condition, d, lines):
+        targets = present(-1) + present(1) + (core != stage_core(d, x)).astype(jnp.int32)
+        ours = condition & (layer_in(d) == 0) & jnp.logical_not(is_source(d))
+        for n in (1, 2, 3):
+            for r in lines:
+                size = bands.at[pl.ds(0, n), pl.ds(0, REACH + r * TERM)]
+                await_sent(ours & (targets == n), size, band_send.at[r])
+
+    whole = bands.at[pl.ds(0, 2), pl.ds(0, REACH + TERM // 2)]
+
+    def await_seconds(d):
+        remote = core != stage_core(d, x)
+        await_sent(remote & (layer_in(d) == 1), whole, band_send.at[2])
+
+    def blocks(n):
+        return arrived.at[0, pl.ds(0, n)]
+
+    def sources(d):
         for s in (-1, 1, 0):
             remote = exists(s) if s else core != stage_core(d, x)
 
             @pl.when(is_source(d) & remote)
             def _():
-                act(
-                    send(
-                        terms.at[OUTGOING + d],
-                        first.at[1 - s],
-                        side_send.at[1 + s],
-                        trace_recv.at[0, 2 - s],
-                        x,
-                        stage_core(d, x),
-                        s,
-                    )
-                )
-
-    def forward(e, act):
+                send(
+                    terms.at[OUTGOING + d],
+                    first.at[1 - s],
+                    side_send,
+                    trace_recv.at[0, 2 - s],
+                    x,
+                    stage_core(d, x),
+                    s,
+                ).start()
+
+    def await_sources(d):
+        targets = present(-1) + present(1) + (core != stage_core(d, x)).astype(jnp.int32)
+        for n in (1, 2, 3):
+            await_sent(is_source(d) & (targets == n), blocks(n), side_send)
+
+    def await_forward(e):
+        for n in (3, 4, 5):
+            await_sent(spread == n, blocks(n), trace_send.at[e])
+        if e == 1:
+            for n in (2, 3):
+                await_sent(reach == n, blocks(n), side_send)
+
+    def forward(e):
         d = (early + e) % 2
         to = x + 1 - 2 * d
         slot = (stage_of(d) + 1) // 2
@@ -328,32 +351,15 @@
             return send(
                 second.at[e],
                 beside.at[1 - s],
-                side_send.at[1 + s],
+                side_send,
                 trace_recv.at[1, 2 - s],
                 to,
                 1 - stage_core(d, to),
                 s,
             )
 
-        if act is wait_send:
-            for n in (3, 4, 5):
-
-                @pl.when(spread == n)
-                def _():
-                    blocks = arrived.at[0, pl.ds(0, n)]
-                    send(blocks, blocks, trace_send.at[e], trace_recv.at[0, 0], x, partner, 0).wait_send()
-
-            if e == 1:
-                for s in (-1, 1, 0):
-
-                    @pl.when(exists(s))
-                    def _():
-                        extra(s).wait_send()
-
-            return
-
         for crossing in (True, False):
-            for copies, reached in ((main, (-1, 1, -2, 2, 0)), (extra, (-1, 1, 0))):
+            for copies, reached in ((main, (-1, 1)), (extra, (-1, 1)), (main, (-2, 2, 0)), (extra, (0,))):
                 if copies is extra and e == 0:
                     continue
                 for s in reached:
@@ -363,13 +369,13 @@
 
                     @pl.when(exists(s) & (side if crossing else jnp.logical_not(side)))
                     def _():
-                        act(copies(s))
+                        copies(s).start()
 
     def hand(e, d, from_second):
         return send(
             second.at[e] if from_second else centre.at[e],
             result.at[d],
-            hand_send.at[e],
+            hand_send,
             hand_recv.at[d],
             x,
             partner,
@@ -403,13 +409,13 @@
 
     @pl.when(collects & (x >= 2))
     def _():
-        pl.semaphore_signal(far, inc=1, device_id=(x * 2 + partner, k), device_id_type=MESH)
-
-    for d in range(2):
-        sources(d, start)
+        pl.semaphore_signal(go, inc=1, device_id=(x * 2 + partner, k), device_id_type=MESH)
+
+    for d in range(2):
+        sources(d)
     for d in range(2):
         for seconds in (False, True):
-            give(event_of(d) == 0, d, start, seconds, (0,))
+            give(event_of(d) == 0, d, seconds, (0,))
 
     @pl.when(jnp.logical_not(origin | patient))
     def _():
@@ -417,11 +423,11 @@
 
     for d in range(2):
         for seconds in (False, True):
-            give(event_of(d) == 0, d, start, seconds, (1,))
+            give(event_of(d) == 0, d, seconds, (1,))
     for r in range(2):
         build(1, r)
     for d in range(2):
-        give(event_of(d) == 1, d, start, True)
+        give(event_of(d) == 1, d, True)
 
     def let_go():
         pl.semaphore_signal(go, inc=1, device_id=(x * 2 + partner, k), device_id_type=MESH)
@@ -429,7 +435,7 @@
     leads = between & (core == early)
     follows = between & (core != early)
     for d in range(2):
-        give(leads & (event_of(d) == 0), d, wait_send, False, (0,))
+        await_given(leads & (event_of(d) == 0), d, (0,))
 
     @pl.when(leads)
     def _():
@@ -440,7 +446,7 @@
         pl.semaphore_wait(go, 1)
 
     for d in range(2):
-        give(follows & (event_of(d) == 1), d, start, False)
+        give(follows & (event_of(d) == 1), d, False)
 
     def event(e):
         d = (early + e) % 2
@@ -457,9 +463,7 @@
 
             @pl.when(here)
             def _():
-                for r in range(2):
-                    piece = bands.at[base + slot, pl.ds(0, REACH + r * TERM)]
-                    await_recv(piece, band_recv.at[base + slot, r])
+                await_recv(whole, band_recv.at[base + slot])
 
         if e == 0:
 
@@ -483,7 +487,6 @@
 
         @pl.when(X >= 1)
         def _():
-            turn = 1 - 2 * (k % PLANE >= PLANE // 2).astype(jnp.int32)
             await_band(SECOND)
             for t in range(3):
                 outer[t] = band_block(bands, base + SECOND, t)
@@ -510,11 +513,11 @@
 
             @pl.when(x >= 2)
             def _():
-                pl.semaphore_wait(far, 1)
+                pl.semaphore_wait(go, 1)
 
         @pl.when(X < 3)
         def _():
-            forward(e, start)
+            forward(e)
 
         @pl.when((X == 1) | (X == 2))
         def _():
@@ -552,25 +555,23 @@
         pl.semaphore_wait(go, 1)
 
     for d in range(2):
-        give(((x == 0) | (x == 3)) & (event_of(d) == 1), d, start, False)
+        give(((x == 0) | (x == 3)) & (event_of(d) == 1), d, False)
 
     late = on_one != (x == 0)
 
     def finish():
         for d in range(2):
-            sources(d, wait_send)
+            await_sources(d)
             led = leads & (event_of(d) == 0)
-            give(led, d, wait_send, False, (1,))
-            give(jnp.logical_not(led), d, wait_send, False)
-            give(True, d, wait_send, True)
+            await_given(led, d, (1,))
+            await_given(jnp.logical_not(led), d, (0, 1))
+            await_seconds(d)
 
         @pl.when(on_one)
         def _():
-            forward(0, wait_send)
-
-            @pl.when(x != 0)
-            def _():
-                hand(0, early, True).wait_send()
+            await_forward(0)
+
+        await_sent(on_one & (x == 3), blocks(1), hand_send)
 
     @pl.when(jnp.logical_not(between))
     def _():
@@ -587,13 +588,15 @@
         def _():
             at = OUTGOING + d
             total = terms[at].astype(F32)
-            for b in (1, 0, 2):
-
-                @pl.when(exists(b - 1))
+            for b in range(3):
+                outer[b] = band_block(bands, at, b)
+            for b in (HOME, 1 + turn, 1 - turn):
+
+                @pl.when((k + b - 1 >= 0) & (k + b - 1 < devices))
                 def _():
                     await_recv(beside.at[b], trace_recv.at[1, 1 + b])
 
-                total = total + times(beside[b], bands, at, b)
+                total = total + times_all(beside[b], outer[b])
             result[d] = total.astype(BF16)
 
         @pl.when(jnp.logical_not(computes(d) | is_source(d) | last))
@@ -608,8 +611,8 @@
 
         @pl.when(late)
         def _():
-            forward(1, wait_send)
-            hand(1, 1 - early, True).wait_send()
+            await_forward(1)
+            await_sent(True, blocks(2), hand_send)
 
 
 def shards(down_sources, up_sources, down_tiles, up_tiles, tile_rows, tile_cols, shot_order):
@@ -643,14 +646,13 @@
             dma((3,)),
             dma,
             dma,
-            dma((4, 2)),
-            dma((OUTGOING, 2)),
             dma((3,)),
+            dma((OUTGOING,)),
+            dma,
             dma((2,)),
             dma((2, 5)),
+            dma,
             dma((2,)),
-            dma((2,)),
-            pltpu.SemaphoreType.REGULAR,
             pltpu.SemaphoreType.REGULAR,
         ],
         compiler_params=pltpu.CompilerParams(collective_id=0, has_side_effects=True),

time: 25.2 us -> 24.8 us (0.984)
  Pallas kernels: 24.5 us -> 24.1 us
    pallas_call x1, Pallas kernels: 24.5 us -> 24.1 us  [shards(): pl.pallas_call(kernel, name='sweeps', out_shape=pltpu.VMEM(down_sources.s...]
where the time goes in v7:
time: 24.8 us; the launch traced here: 24.7 us
  Pallas kernels  24.1 us (97%)
  local copies, waits for them, and re-layouts  0.61 us (2%)
    pallas_call x1, Pallas kernels, shards(): pl.pallas_call(kernel, name='sweeps', out_shape=pltpu.VMEM(down_sources.s...  24.1 us
    unnamed x1, local copies, waits for them, and re-layouts  0.61 us

profile of v7, /device:TPU:385, one launch (start us, length us, event | category | flops | bytes accessed | tf_op | source)
XLA Modules:
  0.0 24.7 jit_solution(5839584003144182735)
XLA Ops:
  0.0 24.1 %sweeps.1 = bf16[1,32,256]{2,1,0:T(8,128)(2,1)S(1)} custom-call(s32[16]{0:T(128)} %bitcast.2, s32[16]{0:T(128)} %bitcast.3, s32[32]{0:T(128)} %order_hbm.1, bf16[1,32,256]{2,1,0:T(8,128)(2,1)} %down_src.1, bf16[1,32,256]{2,1,0:T(8,128)(2,1)} %up_src.1, bf16[1,16,128,128]{3,2,1,0:T(8,128)(2,1)} %down_tiles.1, bf16[1,16,128,128]{3,2,1,0:T(8,128)(2,1)} %up_tiles.1), custom_call_target="tpu_custom_call" | custom-call | tf_op jit(solution)/shard_map/sweeps/pallas_call | solution.py:623
  24.1 0.6 %copy.9 = bf16[1,32,256]{2,1,0:T(8,128)(2,1)} copy(bf16[1,32,256]{2,1,0:T(8,128)(2,1)S(1)} %sweeps.1) | data formatting | bytes 32768

commit v8 on v7

--- a/solution.py
+++ b/solution.py
@@ -444,6 +444,7 @@
     @pl.when(follows)
     def _():
         pl.semaphore_wait(go, 1)
+        pl.delay(1300)
 
     for d in range(2):
         give(follows & (event_of(d) == 1), d, False)
@@ -471,13 +472,15 @@
             def _():
                 await_band(SECOND)
                 total = terms[base + SECOND].astype(F32)
-                for b in (1, 0, 2):
-
-                    @pl.when(exists(b - 1) if b != 1 else d == 0)
+                for b in range(3):
+                    outer[b] = band_block(bands, base + SECOND, b)
+                for b in (HOME, 1 + turn, 1 - turn):
+
+                    @pl.when(d == 0 if b is HOME else (k + b - 1 >= 0) & (k + b - 1 < devices))
                     def _():
                         await_recv(first.at[b], trace_recv.at[0, 1 + b])
 
-                    total = total + times(first[b], bands, base + SECOND, b)
+                    total = total + times_all(first[b], outer[b])
                 second[e] = total.astype(BF16)
 
         def await_block(block):

time: 24.8 us -> 24.6 us (level)
  Pallas kernels: 24.1 us -> 23.8 us
    pallas_call x1, Pallas kernels: 24.1 us -> 23.8 us  [shards(): pl.pallas_call(kernel, name='sweeps', out_shape=pltpu.VMEM(down_sources.s...]
where the time goes in v8:
time: 24.6 us; the launch traced here: 24.4 us
  Pallas kernels  23.8 us (97%)
  local copies, waits for them, and re-layouts  0.61 us (2%)
    pallas_call x1, Pallas kernels, shards(): pl.pallas_call(kernel, name='sweeps', out_shape=pltpu.VMEM(down_sources.s...  23.8 us
    unnamed x1, local copies, waits for them, and re-layouts  0.61 us

profile of v8, /device:TPU:385, one launch (start us, length us, event | category | flops | bytes accessed | tf_op | source)
XLA Modules:
  0.0 24.4 jit_solution(16263575209929823088)
XLA Ops:
  0.0 23.8 %sweeps.1 = bf16[1,32,256]{2,1,0:T(8,128)(2,1)S(1)} custom-call(s32[16]{0:T(128)} %bitcast.2, s32[16]{0:T(128)} %bitcast.3, s32[32]{0:T(128)} %order_hbm.1, bf16[1,32,256]{2,1,0:T(8,128)(2,1)} %down_src.1, bf16[1,32,256]{2,1,0:T(8,128)(2,1)} %up_src.1, bf16[1,16,128,128]{3,2,1,0:T(8,128)(2,1)} %down_tiles.1, bf16[1,16,128,128]{3,2,1,0:T(8,128)(2,1)} %up_tiles.1), custom_call_target="tpu_custom_call" | custom-call | tf_op jit(solution)/shard_map/sweeps/pallas_call | solution.py:626
  23.8 0.6 %copy.9 = bf16[1,32,256]{2,1,0:T(8,128)(2,1)} copy(bf16[1,32,256]{2,1,0:T(8,128)(2,1)S(1)} %sweeps.1) | data formatting | bytes 32768

commit v9 on v8

--- a/solution.py
+++ b/solution.py
@@ -444,7 +444,13 @@
     @pl.when(follows)
     def _():
         pl.semaphore_wait(go, 1)
-        pl.delay(1300)
+        @pl.when(x == 1)
+        def _():
+            pl.delay(1000)
+
+        @pl.when(x == 2)
+        def _():
+            pl.delay(1700)
 
     for d in range(2):
         give(follows & (event_of(d) == 1), d, False)

time: 24.6 us -> 24.7 us (level)
  no operation moved by 1% of the time
where the time goes in v9:
time: 24.7 us; the launch traced here: 24.5 us
  Pallas kernels  23.8 us (96%)
  local copies, waits for them, and re-layouts  0.61 us (2%)
    pallas_call x1, Pallas kernels, shards(): pl.pallas_call(kernel, name='sweeps', out_shape=pltpu.VMEM(down_sources.s...  23.8 us
    unnamed x1, local copies, waits for them, and re-layouts  0.61 us

profile of v9, /device:TPU:385, one launch (start us, length us, event | category | flops | bytes accessed | tf_op | source)
XLA Modules:
  0.0 24.5 jit_solution(16462129031661019302)
XLA Ops:
  0.0 23.8 %sweeps.1 = bf16[1,32,256]{2,1,0:T(8,128)(2,1)S(1)} custom-call(s32[16]{0:T(128)} %bitcast.2, s32[16]{0:T(128)} %bitcast.3, s32[32]{0:T(128)} %order_hbm.1, bf16[1,32,256]{2,1,0:T(8,128)(2,1)} %down_src.1, bf16[1,32,256]{2,1,0:T(8,128)(2,1)} %up_src.1, bf16[1,16,128,128]{3,2,1,0:T(8,128)(2,1)} %down_tiles.1, bf16[1,16,128,128]{3,2,1,0:T(8,128)(2,1)} %up_tiles.1), custom_call_target="tpu_custom_call" | custom-call | tf_op jit(solution)/shard_map/sweeps/pallas_call | solution.py:632
  23.8 0.6 %copy.9 = bf16[1,32,256]{2,1,0:T(8,128)(2,1)} copy(bf16[1,32,256]{2,1,0:T(8,128)(2,1)S(1)} %sweeps.1) | data formatting | bytes 32768

commit v10 on v8

--- a/solution.py
+++ b/solution.py
@@ -557,6 +557,10 @@
     def _():
         pl.semaphore_wait(go, 1)
 
+    @pl.when(((x == 0) & on_one) | ((x == 3) & jnp.logical_not(on_one)))
+    def _():
+        pl.delay(1500)
+
     for d in range(2):
         give(((x == 0) | (x == 3)) & (event_of(d) == 1), d, False)
 

time: 24.6 us -> 24.6 us (level)
  no operation moved by 1% of the time
where the time goes in v10:
time: 24.6 us; the launch traced here: 24.4 us
  Pallas kernels  23.8 us (97%)
  local copies, waits for them, and re-layouts  0.61 us (2%)
    pallas_call x1, Pallas kernels, shards(): pl.pallas_call(kernel, name='sweeps', out_shape=pltpu.VMEM(down_sources.s...  23.8 us
    unnamed x1, local copies, waits for them, and re-layouts  0.61 us

profile of v10, /device:TPU:385, one launch (start us, length us, event | category | flops | bytes accessed | tf_op | source)
XLA Modules:
  0.0 24.4 jit_solution(8802666128731865065)
XLA Ops:
  0.0 23.8 %sweeps.1 = bf16[1,32,256]{2,1,0:T(8,128)(2,1)S(1)} custom-call(s32[16]{0:T(128)} %bitcast.2, s32[16]{0:T(128)} %bitcast.3, s32[32]{0:T(128)} %order_hbm.1, bf16[1,32,256]{2,1,0:T(8,128)(2,1)} %down_src.1, bf16[1,32,256]{2,1,0:T(8,128)(2,1)} %up_src.1, bf16[1,16,128,128]{3,2,1,0:T(8,128)(2,1)} %down_tiles.1, bf16[1,16,128,128]{3,2,1,0:T(8,128)(2,1)} %up_tiles.1), custom_call_target="tpu_custom_call" | custom-call | tf_op jit(solution)/shard_map/sweeps/pallas_call | solution.py:630
  23.8 0.6 %copy.9 = bf16[1,32,256]{2,1,0:T(8,128)(2,1)} copy(bf16[1,32,256]{2,1,0:T(8,128)(2,1)S(1)} %sweeps.1) | data formatting | bytes 32768
